TPU v7x, 32 devices: a whole 2x2x4 slice. The times are simulated.
32 devices in a mesh: seq: 8 (over z, x), head: 4 (over y, core).
Axes of the slice: x: 2, y: 2, z: 4, core: 2. Of those that a mesh axis runs over, the one named last changes fastest.
Arguments:
- tokens: bfloat16 [1024, 2048], P('seq', 'head'), may hold values from -6 to 6
- norm_gain: float32 [2048], replicated, may hold values from 0.1 to 1.9
- query_weight: bfloat16 [2048, 2048], P(None, 'head')
- key_weight: bfloat16 [2048, 256], replicated, may hold values from -0.125 to 0.125
- value_weight: bfloat16 [2048, 256], replicated, may hold values from -0.125 to 0.125
- window_lengths: int32 [8], replicated, may hold values from 1 to 256, 1024 in all
- is_caption: int32 [1024], P('seq'), may hold values 0 or 1
- span_blocks: int32 [8, 2], P('seq'), may hold values from 0 to 7, as said below
Outputs:
- attended: bfloat16 [1024, 2048], P('seq', 'head')
Inputs may be any that keep to these rules, and one draw needn't show every extreme that they name: `window_lengths`: window lengths are whole numbers summing to 1024, the largest exactly 256. `is_caption`: 1 marks a caption token, 0 a visual token. `span_blocks`: row b holds first and last key block of one event span: first <= last <= first + 1 and first <= 6; some span has exactly 2 blocks.
All inputs are finite; a program needn't handle non-finite values. No bound on the sum of `is_caption` on one device may be relied on, other than what follows from the above.
Results may differ from a plain program's by a relative error of at most 0.019.
The roundings to bfloat16 on the way count: a program that leaves them out, or rounds other values in their place, can miss the bound.
Values may be sent and summed in bfloat16 or wider, within the bound.
No kernel may reach another device: no remote copies, remote signals or barrier semaphores. Data moves between devices by JAX's collectives and lax.ppermute only.
A program may use at most 64 MiB of HBM per device.

v0:
```python
import jax
import jax.numpy as jnp
from jax import lax
from jax.sharding import PartitionSpec as P

H = 16
KV = 2
HD = 128
BLOCK = 128


norm_eps = 1e-05
rope_base = 500000.0
window_cap = 4096
span_cap = 8
slice_blocks = 8
lowest_start = -1e30


def rotate(vectors, position):
    half_size = vectors.shape[-1] // 2
    frequency = rope_base ** (-jnp.arange(half_size, dtype=jnp.float32) * 2.0 / vectors.shape[-1])
    angles = position.astype(jnp.float32)[:, None] * frequency[None, :]
    cosine = jnp.cos(angles)[:, None, :]
    sine_part = jnp.sin(angles)[:, None, :]
    first_half = vectors[..., :half_size]
    second_half = vectors[..., half_size:]
    return jnp.concatenate(
        [
            first_half * cosine - second_half * sine_part,
            second_half * cosine + first_half * sine_part,
        ],
        -1,
    )


def rms_normed(tokens, norm_gain):
    hidden = tokens.astype(jnp.float32)
    scale = lax.rsqrt(jnp.mean(hidden * hidden, -1, keepdims=True) + norm_eps)
    return (hidden * scale * norm_gain[None, :]).astype(jnp.bfloat16)


def window_starts(window_lengths, position):
    window_ends = jnp.cumsum(window_lengths)
    begins = window_ends - window_lengths
    within = (begins[None, :] <= position[:, None]) & (position[:, None] < window_ends[None, :])
    return jnp.sum(jnp.where(within, begins[None, :], 0), 1)


def inside(first_row, row_pos, key_pos):
    return (first_row[:, None] <= key_pos[None, :]) & (key_pos[None, :] <= row_pos[:, None])


def absorb(softmax_state, queries, key_values, allowed):
    highest, denominator, weighted = softmax_state
    head_size = queries.shape[-1]
    scores = jnp.einsum(
        "rhd,nd->rhn", queries, key_values[:, :head_size], preferred_element_type=jnp.float32
    )
    scores = jnp.where(allowed[:, None, :], scores, -jnp.inf)
    updated = jnp.maximum(highest, jnp.max(scores, -1))
    rescale = jnp.exp(highest - updated)
    weights = jnp.exp(scores - updated[..., None])
    denominator = rescale * denominator + jnp.sum(weights, -1)
    weighted = rescale[..., None] * weighted + jnp.einsum(
        "rhn,nd->rhd",
        weights.astype(jnp.bfloat16),
        key_values[:, head_size:],
        preferred_element_type=jnp.float32,
    )
    return (updated, denominator, weighted)


def absorb_sliced(softmax_state, queries, key_values, allowed):
    key_count = key_values.shape[0]
    piece = slice_blocks * BLOCK
    for begin in range(0, key_count, piece):
        finish = min(begin + piece, key_count)
        softmax_state = absorb(
            softmax_state, queries, key_values[begin:finish], allowed[:, begin:finish]
        )
    return softmax_state


def select(layout, wanted, total_blocks):
    blocks_dev = layout.shape[0]
    clipped = jnp.clip(wanted, 0, total_blocks - 1)
    return layout[clipped % blocks_dev, clipped // blocks_dev]


def per_device(
    tokens,
    norm_gain,
    query_weight,
    key_weight,
    value_weight,
    window_lengths,
    is_caption,
    span_blocks,
):
    ranks = lax.axis_size("seq")
    device_rank = lax.axis_index("seq")
    features = lax.all_gather(tokens, "head", axis=1, tiled=True)
    local_rows = features.shape[0]
    blocks_dev = local_rows // BLOCK
    total_blocks = blocks_dev * ranks
    window = min(window_cap, total_blocks * BLOCK // 4)
    span_most = min(span_cap, total_blocks // 4)
    window_back = (window + BLOCK - 2) // BLOCK
    first_pos = device_rank * local_rows
    row_pos = first_pos + jnp.arange(local_rows, dtype=jnp.int32)
    normed = rms_normed(features, norm_gain)
    head_dev = query_weight.shape[1] // HD
    kv_index = lax.axis_index("head") * head_dev // (H // KV)
    queries = jnp.dot(normed, query_weight, preferred_element_type=jnp.float32).reshape(
        local_rows, head_dev, HD
    )
    queries = (rotate(queries, row_pos) * HD ** (-0.5)).astype(jnp.bfloat16)
    key_columns = lax.dynamic_slice_in_dim(key_weight, kv_index * HD, HD, 1)
    value_columns = lax.dynamic_slice_in_dim(value_weight, kv_index * HD, HD, 1)
    key_rows = jnp.dot(normed, key_columns, preferred_element_type=jnp.float32).reshape(
        local_rows, 1, HD
    )
    key_rows = rotate(key_rows, row_pos).reshape(local_rows, HD).astype(jnp.bfloat16)
    value_rows = jnp.dot(normed, value_columns, preferred_element_type=jnp.float32).astype(
        jnp.bfloat16
    )
    key_values = jnp.concatenate([key_rows, value_rows], 1)
    window_first = window_starts(window_lengths, row_pos)
    caption_rows = is_caption == 1
    row_block = jnp.arange(local_rows, dtype=jnp.int32) // BLOCK
    span_end = span_blocks[:, 1][row_block]
    all_spans = lax.all_gather(span_blocks, "seq", axis=0, tiled=True)
    pieces = key_values.reshape(blocks_dev, ranks, BLOCK // ranks, 2 * HD)
    layout = lax.all_to_all(pieces, "seq", split_axis=1, concat_axis=1, tiled=True)
    offsets = jnp.arange(span_most, dtype=jnp.int32)
    span_wanted = all_spans[:, 0].reshape(ranks, blocks_dev, 1) + offsets[None, None, :]
    span_wanted = span_wanted.reshape(ranks, blocks_dev * span_most).T
    own_starts = span_blocks[:, 0]
    span_pos = (
        (own_starts[:, None] + offsets[None, :])[:, :, None] * BLOCK
        + jnp.arange(BLOCK, dtype=jnp.int32)[None, None, :]
    ).reshape(-1)
    span_owner = jnp.arange(blocks_dev * span_most * BLOCK, dtype=jnp.int32) // (span_most * BLOCK)
    span_ok = (span_owner[None, :] == row_block[:, None]) & (
        span_pos[None, :] // BLOCK <= span_end[:, None]
    )
    span_ok = span_ok & caption_rows[:, None] & ~inside(window_first, row_pos, span_pos)
    start_state = (
        jnp.full((local_rows, head_dev), lowest_start, jnp.float32),
        jnp.zeros((local_rows, head_dev), jnp.float32),
        jnp.zeros((local_rows, head_dev, HD), jnp.float32),
    )
    near_index = jnp.arange(window_back + blocks_dev, dtype=jnp.int32)
    near_wanted = (
        (jnp.arange(ranks, dtype=jnp.int32) * blocks_dev)[None, :]
        - window_back
        + near_index[:, None]
    )
    wanted = jnp.concatenate([near_wanted, span_wanted], 0)
    delivered = lax.all_to_all(
        select(layout, wanted, total_blocks), "seq", split_axis=1, concat_axis=1, tiled=True
    )
    gathered = delivered.reshape(-1, 2 * HD)
    near_pos = (first_pos // BLOCK - window_back) * BLOCK + jnp.arange(
        (window_back + blocks_dev) * BLOCK, dtype=jnp.int32
    )
    allowed = jnp.concatenate([inside(window_first, row_pos, near_pos), span_ok], 1)
    softmax_state = absorb_sliced(start_state, queries, gathered, allowed)
    highest, denominator, weighted = softmax_state
    return (
        (weighted / denominator[..., None]).reshape(local_rows, head_dev * HD).astype(jnp.bfloat16)
    )


def solution(mesh):
    in_specs = (P("seq", "head"), P(), P(None, "head"), P(), P(), P(), P("seq"), P("seq", None))
    out_specs = P("seq", "head")
    return jax.shard_map(
        per_device, mesh=mesh, in_specs=in_specs, out_specs=out_specs, check_vma=False
    )
```

profile of v0, /device:TPU:0, one launch (start us, length us, event | category | flops | bytes accessed | tf_op | source)
XLA Modules:
  0.0 59.4 jit_solution(15557514870400121325)
XLA Ops:
  0.0 0.0 copy-start
  0.0 0.0 copy-start.1
  0.1 9.0 %all_gather.6 = bf16[128,2048]{1,0:T(8,128)(2,1)S(1)} all-gather(bf16[128,512]{1,0:T(8,128)(2,1)} %param.8), channel_id=1, replica_groups=mesh['seq'=8,'head'=4] {'head'}, dimensions={1}, use_global_device_ids=true | all-gather | bytes 655360 | tf_op jit(solution)/shard_map/all_gather | solution.py:103
  9.1 0.2 fusion.4
  9.3 0.0 copy-start.3
  9.3 0.0 copy-start.4
  9.3 0.0 copy-start.2
  9.3 1.5 %convolution_convert_fusion = bf16[128,128]{0,1:T(8,128)(2,1)S(1)} fusion(bf16[2048,256]{1,0:T(8,128)(2,1)} %param.12, s32[]{:T(128)S(6)} %select_n.76, bf16[128,2048]{1,0:T(8,128)(2,1)S(1)} %all_gather.6, f32[2048]{0:T(1024)} %param.9, f32[128]{0:T(128)S(1)} %add_rsqrt_fusion), kind=kOutput, calls=%fused_computation.11 | convolution fusion | flops 68173824 | bytes 1090052 | tf_op jit(solution)/shard_map/dot_general | solution.py:125
  10.8 0.0 copy-done.1
  10.8 1.5 %convolution_bitcast_fusion = f32[128,1,128]{0,2,1:T(8,128)S(1)} fusion(bf16[2048,256]{1,0:T(8,128)(2,1)} %param.11, s32[]{:T(128)S(6)} %select_n.76, bf16[128,2048]{1,0:T(8,128)(2,1)S(1)} %all_gather.6, f32[2048]{0:T(1024)S(1)} %copy-done.1, f32[128]{0:T(128)S(1)} %add_rsqrt_fusion), kind=kOutput, calls=%fused_computation.10 | convolution fusion | flops 68157440 | bytes 1122820 | tf_op jit(solution)/shard_map/dot_general | solution.py:121
  12.3 0.2 fusion.19
  12.5 0.7 %copy.33 = bf16[128,256]{1,0:T(8,128)(2,1)} copy(bf16[128,256]{0,1:T(8,128)(2,1)S(1)} %pad_maximum_fusion) | data formatting | bytes 131072 | tf_op jit(solution)/shard_map/concatenate | solution.py:128
  13.2 5.8 %all-to-all-start = ((bf16[1,8,16,256]{3,2,0,1:T(8,128)(2,1)}), bf16[1,8,16,256]{3,2,0,1:T(8,128)(2,1)S(1)}, u32[]{:S(2)}, u32[]{:S(2)}) async-start(bf16[1,8,16,256]{3,2,0,1:T(8,128)(2,1)} %bitcast.9), calls=%async_computation | async-start | bytes 131072 | tf_op jit(solution)/shard_map/all_to_all | solution.py:135
  19.1 0.3 multiply_cosine_fusion
  19.4 0.0 copy-done.3
  19.4 0.2 reduce-window.8
  19.6 0.0 copy-done.4
  19.6 0.0 copy-done.2
  19.6 0.6 %fusion.36 = (s32[1,1]{1,0:T(1,128)}, s32[1,1]{1,0:T(1,128)}) fusion(s32[1,2]{1,0:T(1,128)S(1)} %copy-done.2), kind=kLoop, calls=%fused_computation.82 | loop fusion | bytes 16 | tf_op jit(solution)/shard_map/slice | solution.py:132
  20.2 0.6 %add_multiply_fusion = s32[2]{0:T(128)S(1)} fusion(s32[]{:T(128)} %bitcast.2), kind=kLoop, calls=%fused_computation.70 | loop fusion | flops 4 | bytes 12 | tf_op jit(solution)/shard_map/mul | solution.py:141
  20.8 0.1 add.213
  20.9 0.6 %fusion.24 = pred[256]{0:T(512)(128)(4,1)S(1)} fusion(s32[]{:T(128)} %bitcast.5, s32[256]{0:T(256)S(1)} %bitcast.47), kind=kLoop, calls=%fused_computation.65 | loop fusion | flops 4352 | bytes 1284 | tf_op jit(solution)/shard_map/le | solution.py:146
  21.6 21.0 %all-gather = s32[8,1,2]{2,1,0:T(1,128)S(1)} all-gather(s32[1,1,2]{2,1,0:T(1,128)S(1)} %bitcast.45), channel_id=1, replica_groups=mesh['seq'=8,'head'=4] {'seq'}, dimensions={0}, use_global_device_ids=true | all-gather | bytes 72 | tf_op jit(solution)/shard_map/all_gather | solution.py:133
  42.5 0.1 copy.35
  42.7 0.1 reshape.403
  42.7 0.0 copy-done
  42.7 0.5 fusion.33
  43.2 0.1 reshape.399
  43.3 0.1 select_reduce_fusion
  43.4 0.1 compare_and_fusion
  43.6 0.1 not_and_fusion
  43.7 0.0 all-to-all-done
  43.7 0.6 %gather_fusion = bf16[40,16,256]{2,1,0:T(8,128)(2,1)S(1)} fusion(bf16[1,8,16,256]{3,2,1,0:T(8,128)(2,1)S(1)} %bitcast.40, s32[40]{0:T(128)S(1)} %reshape.403), kind=kCustom, calls=%fused_computation | custom fusion | bytes 655680 | tf_op jit(solution)/shard_map/gather | solution.py:88
  44.3 0.7 %copy.37 = bf16[5,8,16,256]{3,2,0,1:T(8,128)(2,1)} copy(bf16[5,8,16,256]{3,2,1,0:T(8,128)(2,1)S(1)} %bitcast.41) | data formatting | bytes 655360 | tf_op jit(solution)/shard_map/gather | solution.py:88
  45.1 3.4 %all-to-all-start.1 = ((bf16[5,8,16,256]{3,2,0,1:T(8,128)(2,1)}), bf16[5,8,16,256]{3,2,0,1:T(8,128)(2,1)S(1)}, u32[]{:S(2)}, u32[]{:S(2)}) async-start(bf16[5,8,16,256]{3,2,0,1:T(8,128)(2,1)} %copy.37), calls=%async_computation.1 | async-start | bytes 655360 | tf_op jit(solution)/shard_map/all_to_all | solution.py:161
  48.6 0.2 fusion.35
  48.8 0.1 multiply_subtract_fusion
  48.8 8.3 %all-to-all-done.1 = bf16[5,8,16,256]{3,2,0,1:T(8,128)(2,1)S(1)} async-done(((bf16[5,8,16,256]{3,2,0,1:T(8,128)(2,1)}), bf16[5,8,16,256]{3,2,0,1:T(8,128)(2,1)S(1)}, u32[]{:S(2)}, u32[]{:S(2)}) %all-to-all-start.1) | async-done | bytes 327712 | tf_op jit(solution)/shard_map/all_to_all | solution.py:161
  57.2 0.5 fusion.37
  57.7 0.4 fusion.1
  58.1 0.5 fusion.3
  58.6 0.8 %copy.40 = bf16[128,512]{1,0:T(8,128)(2,1)} copy(bf16[128,512]{0,1:T(8,128)(2,1)S(1)} %bitcast.44) | data formatting | bytes 262144 | tf_op jit(solution)/shard_map/convert_element_type | solution.py:172
  (19 shorter events, 0.2 us)
Async XLA Ops:
  0.0 42.7 %copy-start = (bf16[2048,512]{1,0:T(8,128)(2,1)S(1)}, bf16[2048,512]{1,0:T(8,128)(2,1)}, u32[]{:S(2)}) copy-start(bf16[2048,512]{1,0:T(8,128)(2,1)} %param.10) | copy-start | bytes 6291460
  0.0 10.8 %copy-start.1 = (f32[2048]{0:T(1024)S(1)}, f32[2048]{0:T(1024)}, u32[]{:S(2)}) copy-start(f32[2048]{0:T(1024)} %param.9) | copy-start | bytes 24580
  9.3 10.1 %copy-start.3 = (s32[8]{0:T(128)S(1)}, s32[8]{0:T(128)}, u32[]{:S(2)}) copy-start(s32[8]{0:T(128)} %param.13) | copy-start | bytes 100
  9.3 10.3 %copy-start.4 = (s32[128]{0:T(128)S(1)}, s32[128]{0:T(128)}, u32[]{:S(2)}) copy-start(s32[128]{0:T(128)} %param.14) | copy-start | bytes 1540
  9.3 10.3 %copy-start.2 = (s32[1,2]{1,0:T(1,128)S(1)}, s32[1,2]{1,0:T(1,128)}, u32[]{:S(2)}) copy-start(s32[1,2]{1,0:T(1,128)} %param.15) | copy-start | bytes 28
  13.2 30.5 %all-to-all-start = ((bf16[1,8,16,256]{3,2,0,1:T(8,128)(2,1)}), bf16[1,8,16,256]{3,2,0,1:T(8,128)(2,1)S(1)}, u32[]{:S(2)}, u32[]{:S(2)}) async-start(bf16[1,8,16,256]{3,2,0,1:T(8,128)(2,1)} %bitcast.9), calls=%async_computation | async-start | bytes 131072 | tf_op jit(solution)/shard_map/all_to_all | solution.py:135
  45.1 12.0 %all-to-all-start.1 = ((bf16[5,8,16,256]{3,2,0,1:T(8,128)(2,1)}), bf16[5,8,16,256]{3,2,0,1:T(8,128)(2,1)S(1)}, u32[]{:S(2)}, u32[]{:S(2)}) async-start(bf16[5,8,16,256]{3,2,0,1:T(8,128)(2,1)} %copy.37), calls=%async_computation.1 | async-start | bytes 655360 | tf_op jit(solution)/shard_map/all_to_all | solution.py:161
where the time goes:
time: 59.8 us; the launch traced here: 59.4 us
  blocking collectives  30 us (50%)
  starting transfers between devices  9.23 us (15%)
  waiting for transfers between devices  8.3 us (14%)
  matrix products  4.45 us (7%)
  local copies, waits for them, and re-layouts  4.08 us (7%)
  other arithmetic  3.04 us (5%)
    all_gather x1, blocking collectives, per_device(): all_spans = lax.all_gather(span_blocks, 'seq', axis=0, tiled=True)  21 us
    all_gather x1, blocking collectives, per_device(): features = lax.all_gather(tokens, 'head', axis=1, tiled=True)  9.02 us
    all_to_all x1, waiting for transfers between devices, per_device(): lax.all_to_all(select(layout, wanted, total_blocks), 'seq', split_axis=1,...  8.3 us
    all_to_all x1, starting transfers between devices, per_device(): lax.all_to_all(pieces, 'seq', split_axis=1, concat_axis=1, tiled=True)  5.8 us
    all_to_all x1, starting transfers between devices, per_device(): lax.all_to_all(select(layout, wanted, total_blocks), 'seq', split_axis=1,...  3.43 us
    dot_general x1, matrix products, per_device(): jnp.dot(normed, value_columns, preferred_element_type=jnp.float32)  1.48 us
    dot_general x1, matrix products, per_device(): jnp.dot(normed, key_columns, preferred_element_type=jnp.float32)  1.45 us
    gather x2, local copies, waits for them, and re-layouts, select(): return layout[clipped % blocks_dev, clipped // blocks_dev]  1.37 us
  transfers between devices with their start and end apart: 2, of which 1 were waited for; matrix products, arithmetic and copies ran while one was open for 6% of the time, Pallas kernels for 0%

commit v1 on v0

--- a/solution.py
+++ b/solution.py
@@ -1,6 +1,10 @@
+import functools
+
 import jax
 import jax.numpy as jnp
 from jax import lax
+from jax.experimental import pallas as pl
+from jax.experimental.pallas import tpu as pltpu
 from jax.sharding import PartitionSpec as P
 
 H = 16
@@ -88,7 +92,7 @@
     return layout[clipped % blocks_dev, clipped // blocks_dev]
 
 
-def per_device(
+def by_request(
     tokens,
     norm_gain,
     query_weight,
@@ -173,9 +177,215 @@
     )
 
 
+def vmem(count):
+    return [pl.BlockSpec(memory_space=pltpu.VMEM)] * count
+
+
+def smem(count):
+    return [pl.BlockSpec(memory_space=pltpu.SMEM)] * count
+
+
+def turn(u, cosine, sine):
+    return u * cosine + pltpu.roll(u, u.shape[-1] // 2, 1) * sine
+
+
+def kv_kernel(
+    place, x0, x1, x2, x3, gain, key_weight, value_weight, cosine, sine, kv_out, normed_out
+):
+    depth = x0.shape[1]
+    parts = (x0, x1, x2, x3)
+    me, kv_col = place[0], pl.multiple_of(place[1], HD)
+    total = None
+    for part in parts:
+        hidden = part[...].astype(jnp.float32)
+        squares = jnp.sum(hidden * hidden, -1, keepdims=True)
+        total = squares if total is None else total + squares
+    scale = lax.rsqrt(total / (depth * len(parts)) + norm_eps)
+    keys = values = None
+    for order, part in enumerate(parts):
+        first = pl.multiple_of(jnp.bitwise_xor(me, order) * depth, depth)
+        span = pl.ds(first, depth)
+        normed = (part[...].astype(jnp.float32) * scale * gain[:, span]).astype(jnp.bfloat16)
+        normed_out[:, span] = normed
+        k = jnp.dot(
+            normed, key_weight[span, pl.ds(kv_col, HD)], preferred_element_type=jnp.float32
+        )
+        v = jnp.dot(
+            normed, value_weight[span, pl.ds(kv_col, HD)], preferred_element_type=jnp.float32
+        )
+        keys = k if keys is None else keys + k
+        values = v if values is None else values + v
+    kv_out[:, :HD] = turn(keys, cosine[...], sine[...]).astype(jnp.bfloat16)
+    kv_out[:, HD:] = values.astype(jnp.bfloat16)
+
+
+def query_kernel(normed, weight, cosine, sine, out):
+    q = jnp.dot(normed[...], weight[...], preferred_element_type=jnp.float32)
+    for begin in range(0, q.shape[1], HD):
+        turned = turn(q[:, begin : begin + HD], cosine[...], sine[...])
+        out[:, begin : begin + HD] = (turned * HD ** (-0.5)).astype(jnp.bfloat16)
+
+
+def attend_kernel(blocks, place, lengths, spans, q, caption, *refs):
+    kv, (out, scores, bias) = refs[:blocks], refs[blocks:]
+    rows = q.shape[0]
+    rank = place[0]
+    row_pos = rank * rows + lax.broadcasted_iota(jnp.int32, (rows, BLOCK), 0)
+    first_row = jnp.zeros((rows, BLOCK), jnp.int32)
+    begin = jnp.int32(0)
+    for w in range(lengths.shape[0]):
+        end = begin + lengths[w]
+        within = (row_pos >= begin) & (row_pos < end)
+        first_row = jnp.where(within, begin, first_row)
+        begin = end
+    is_caption = jnp.broadcast_to(caption[...], (rows, BLOCK)) == 1
+    for order in range(blocks):
+        block = jnp.bitwise_xor(rank, order)
+        key_pos = block * BLOCK + lax.broadcasted_iota(jnp.int32, (rows, BLOCK), 1)
+        near = (first_row <= key_pos) & (key_pos <= row_pos)
+        reached = (spans[0, 0] <= block) & (block <= spans[0, 1])
+        allowed = near | (is_caption & reached)
+        bias[:, order * BLOCK : (order + 1) * BLOCK] = jnp.where(allowed, 0.0, -jnp.inf)
+    for head in range(q.shape[1] // HD):
+        qh = q[:, head * HD : (head + 1) * HD]
+        for order in range(blocks):
+            columns = slice(order * BLOCK, (order + 1) * BLOCK)
+            scores[:, columns] = (
+                lax.dot_general(
+                    qh,
+                    kv[order][:, :HD],
+                    (((1,), (1,)), ((), ())),
+                    preferred_element_type=jnp.float32,
+                )
+                + bias[:, columns]
+            )
+        s = scores[...]
+        highest = jnp.max(s, -1, keepdims=True)
+        weights = jnp.exp(s - highest)
+        denominator = jnp.sum(weights, -1, keepdims=True)
+        rounded = weights.astype(jnp.bfloat16)
+        mixed = None
+        for order in range(blocks):
+            part = jnp.dot(
+                rounded[:, order * BLOCK : (order + 1) * BLOCK],
+                kv[order][:, HD:],
+                preferred_element_type=jnp.float32,
+            )
+            mixed = part if mixed is None else mixed + part
+        out[:, head * HD : (head + 1) * HD] = (mixed / denominator).astype(jnp.bfloat16)
+
+
+def everywhere(
+    tokens,
+    norm_gain,
+    query_weight,
+    key_weight,
+    value_weight,
+    window_lengths,
+    is_caption,
+    span_blocks,
+):
+    ranks, groups = lax.axis_size("seq"), lax.axis_size("head")
+    rank, group = lax.axis_index("seq"), lax.axis_index("head")
+    rows = tokens.shape[0]
+    head_dev = query_weight.shape[1] // HD
+
+    def pairs(shift):
+        return [
+            (r * groups + g, (r ^ shift(g)[0]) * groups + (g ^ shift(g)[1]))
+            for r in range(ranks)
+            for g in range(groups)
+        ]
+
+    def move(array, shift):
+        return lax.ppermute(array, ("seq", "head"), pairs(shift))
+
+    across = move(tokens, lambda g: (0, 2))
+    beside = move(tokens, lambda g: (0, 1))
+    half = HD // 2
+    frequency = rope_base ** (-jnp.arange(half, dtype=jnp.float32) * 2.0 / HD)
+    row_pos = rank * rows + jnp.arange(rows, dtype=jnp.int32)
+    angles = row_pos.astype(jnp.float32)[:, None] * frequency[None, :]
+    cosine = jnp.tile(jnp.cos(angles), (1, 2))
+    sine = jnp.sin(angles)
+    sine = jnp.concatenate([-sine, sine], 1)
+    corner = move(across, lambda g: (0, 1))
+
+    kv_index = group * head_dev // (H // KV)
+    key_values, normed = pl.pallas_call(
+        kv_kernel,
+        out_shape=(
+            jax.ShapeDtypeStruct((rows, 2 * HD), jnp.bfloat16),
+            jax.ShapeDtypeStruct((rows, query_weight.shape[0]), jnp.bfloat16),
+        ),
+        in_specs=smem(1) + vmem(9),
+        out_specs=tuple(vmem(2)),
+        name="keys_values",
+    )(
+        jnp.stack([group, kv_index * HD]),
+        tokens,
+        beside,
+        across,
+        corner,
+        norm_gain[None, :],
+        key_weight,
+        value_weight,
+        cosine,
+        sine,
+    )
+
+    blocks = {0: key_values}
+    far = ranks // 2
+    plan = [(far, far | 2), (far | 1, far | 3), (2, 1)]
+    fetched = [
+        (both, move(key_values, lambda g, both=both: (both[g % 2], 0))) for both in plan
+    ]
+    last = move(key_values, lambda g: (3, 0))
+    queries = pl.pallas_call(
+        query_kernel,
+        out_shape=jax.ShapeDtypeStruct((rows, head_dev * HD), jnp.bfloat16),
+        in_specs=vmem(4),
+        out_specs=vmem(1)[0],
+        name="queries",
+    )(normed, query_weight, cosine, sine)
+    odd = group % 2 == 1
+    held = {0: key_values, 3: last}
+    for both, own in fetched:
+        other = move(own, lambda g: (0, 1))
+        held[both[0]] = jnp.where(odd, other, own)
+        held[both[1]] = jnp.where(odd, own, other)
+    return pl.pallas_call(
+        functools.partial(attend_kernel, ranks),
+        out_shape=jax.ShapeDtypeStruct((rows, head_dev * HD), jnp.bfloat16),
+        in_specs=smem(3) + vmem(2 + ranks),
+        out_specs=vmem(1)[0],
+        scratch_shapes=[
+            pltpu.VMEM((rows, ranks * BLOCK), jnp.float32),
+            pltpu.VMEM((rows, ranks * BLOCK), jnp.float32),
+        ],
+        name="attend",
+    )(
+        rank[None],
+        window_lengths,
+        span_blocks,
+        queries,
+        is_caption[:, None],
+        *[held[order] for order in range(ranks)],
+    )
+
+
 def solution(mesh):
+    ranks, groups = mesh.shape["seq"], mesh.shape["head"]
     in_specs = (P("seq", "head"), P(), P(None, "head"), P(), P(), P(), P("seq"), P("seq", None))
     out_specs = P("seq", "head")
+
+    def per_device(*arguments):
+        rows = arguments[0].shape[0]
+        head_dev = arguments[2].shape[1] // HD
+        shared = (H // KV) % (2 * head_dev) == 0
+        whole = ranks == 8 and groups == 4 and rows == BLOCK and shared
+        return (everywhere if whole else by_request)(*arguments)
+
     return jax.shard_map(
         per_device, mesh=mesh, in_specs=in_specs, out_specs=out_specs, check_vma=False
     )

time: 59.8 us -> 32.2 us (0.54)
  blocking collectives: 30 us -> 0 us
  Pallas kernels: 0 us -> 9.93 us
  matrix products: 4.45 us -> 0 us
  waiting for transfers between devices: 8.3 us -> 4.99 us
  starting transfers between devices: 9.23 us -> 10.5 us
  local copies, waits for them, and re-layouts: 4.08 us -> 2.85 us
  other arithmetic: 3.04 us -> 3.69 us
    all_gather x2 -> x0, blocking collectives: 30 us -> none  [the longest x1 21 us: per_device(): all_spans = lax.all_gather(span_blocks, 'seq', axis=0, tiled=True)]
    ppermute x0 -> x10, starting transfers between devices: none -> 10.5 us  [move(): return lax.ppermute(array, ('seq', 'head'), pairs(shift))]
    pallas_call x0 -> x3, Pallas kernels: none -> 9.93 us  [the longest x1 3.98 us: everywhere(): pl.pallas_call(functools.partial(attend_kernel, ranks), out_shape=jax.Sha...]
    all_to_all x2 -> x0, starting transfers between devices: 9.23 us -> none  [the longest x1 5.8 us: per_device(): lax.all_to_all(pieces, 'seq', split_axis=1, concat_axis=1, tiled=True)]
    all_to_all x2 -> x0, waiting for transfers between devices: 8.3 us -> none  [the longest x1 8.3 us: per_device(): lax.all_to_all(select(layout, wanted, total_blocks), 'seq', split_axis=1,...]
    ppermute x0 -> x10, waiting for transfers between devices: none -> 4.99 us  [move(): return lax.ppermute(array, ('seq', 'head'), pairs(shift))]
    dot_general x5 -> x0, matrix products: 4.45 us -> none  [the longest x1 1.48 us: per_device(): jnp.dot(normed, value_columns, preferred_element_type=jnp.float32)]
    select_n x2 -> x3, other arithmetic: 0.01 us -> 2.01 us  [the longest x2 1.33 us: everywhere(): held[both[1]] = jnp.where(odd, own, other)]
  transfers between devices with their start and end apart: 2 -> 10, of which waited for: 1 -> 2; matrix products, arithmetic and copies ran while one was open for 6% -> 16% of each run, Pallas kernels for 0% -> 9%
where the time goes in v1:
time: 32.2 us; the launch traced here: 32 us
  starting transfers between devices  10.5 us (33%)
  Pallas kernels  9.93 us (31%)
  waiting for transfers between devices  4.99 us (15%)
  other arithmetic  3.69 us (11%)
  local copies, waits for them, and re-layouts  2.85 us (9%)
    ppermute x10, starting transfers between devices, move(): return lax.ppermute(array, ('seq', 'head'), pairs(shift))  10.5 us
    ppermute x10, waiting for transfers between devices, move(): return lax.ppermute(array, ('seq', 'head'), pairs(shift))  4.99 us
    pallas_call x1, Pallas kernels, everywhere(): pl.pallas_call(functools.partial(attend_kernel, ranks), out_shape=jax.Sha...  3.98 us
    pallas_call x1, Pallas kernels, everywhere(): pl.pallas_call(kv_kernel, out_shape=(jax.ShapeDtypeStruct((rows, 2 * HD),...  3.07 us
    pallas_call x1, Pallas kernels, everywhere(): pl.pallas_call(query_kernel, out_shape=jax.ShapeDtypeStruct((rows, head_d...  2.88 us
    select_n x2, other arithmetic, everywhere(): held[both[1]] = jnp.where(odd, own, other)  1.33 us
    unnamed x10, local copies, waits for them, and re-layouts  1.3 us
    broadcast_in_dim x1, local copies, waits for them, and re-layouts, everywhere(): is_caption[:, None]  0.75 us
  transfers between devices with their start and end apart: 10, of which 2 were waited for; matrix products, arithmetic and copies ran while one was open for 16% of the time, Pallas kernels for 9%

profile of v1, /device:TPU:0, one launch (start us, length us, event | category | flops | bytes accessed | tf_op | source)
XLA Modules:
  0.0 32.0 jit_solution(13279510628102834562)
XLA Ops:
  0.0 0.0 copy-start.4
  0.0 0.5 %collective-permute-start = (bf16[128,512]{1,0:T(8,128)(2,1)}, bf16[128,512]{1,0:T(8,128)(2,1)S(1)}, u32[]{:S(2)}, u32[]{:S(2)}) collective-permute-start(bf16[128,512]{1,0:T(8,128)(2,1)} %x0.1), channel_id=1, source_target_pairs={{0,1},{1,0},{2,3},{3,2},{4,5},{5,4},{6,7},{7,6},{8,9},{9,8},{10,11... | collective-permute-start | bytes 393224 | tf_op jit(solution)/shard_map/ppermute | solution.py:301
  0.5 2.6 %collective-permute-start.1 = (bf16[128,512]{1,0:T(8,128)(2,1)}, bf16[128,512]{1,0:T(8,128)(2,1)S(1)}, u32[]{:S(2)}, u32[]{:S(2)}) collective-permute-start(bf16[128,512]{1,0:T(8,128)(2,1)} %x0.1), channel_id=1, source_target_pairs={{0,2},{1,3},{2,0},{3,1},{4,6},{5,7},{6,4},{7,5},{8,10},{9,11},{10,... | collective-permute-start | bytes 393224 | tf_op jit(solution)/shard_map/ppermute | solution.py:301
  3.1 0.3 fusion
  3.4 4.0 %collective-permute-done.1.x2 = bf16[128,512]{1,0:T(8,128)(2,1)S(1)} collective-permute-done((bf16[128,512]{1,0:T(8,128)(2,1)}, bf16[128,512]{1,0:T(8,128)(2,1)S(1)}, u32[]{:S(2)}, u32[]{:S(2)}) %collective-permute-start.1) | collective-permute-done | bytes 131104 | tf_op jit(solution)/shard_map/ppermute | solution.py:301
  7.4 0.0 copy-start.1
  7.4 0.0 collective-permute-start.2
  7.4 0.7 %pad_add_fusion.place = s32[2]{0:T(128)} fusion(s32[1]{0:T(128)} %bitcast.2, s32[1]{0:T(128)} %bitcast.1), kind=kLoop, calls=%fused_computation.10 | loop fusion | flops 2 | bytes 16 | tf_op jit(solution)/shard_map/stack | solution.py:325
  8.0 0.1 copy.15
  8.1 0.7 %copy.16.cosine = f32[128,128]{1,0:T(8,128)} copy(f32[128,128]{0,1:T(8,128)S(1)} %bitcast.6) | data formatting | bytes 131072 | tf_op jit(solution)/shard_map/tile | solution.py:309
  8.8 0.7 %pad_maximum_fusion.sine = f32[128,128]{1,0:T(8,128)} fusion(f32[128,64]{1,0:T(8,128)S(1)} %get-tuple-element.16, f32[128,64]{1,0:T(8,128)S(1)} %get-tuple-element.15), kind=kLoop, calls=%fused_computation.2 | loop fusion | flops 16384 | bytes 131072 | tf_op jit(solution)/shard_map/concatenate | solution.py:311
  9.5 0.0 collective-permute-done.x1
  9.6 0.0 copy-start
  9.6 0.0 collective-permute-done.2.x3
  9.6 0.0 copy-start.2
  9.6 0.0 copy-done.1
  9.6 0.6 %copy-done = bf16[128,512]{1,0:T(8,128)(2,1)} copy-done((bf16[128,512]{1,0:T(8,128)(2,1)}, bf16[128,512]{1,0:T(8,128)(2,1)S(1)}, u32[]{:S(2)}) %copy-start) | copy-done | bytes 131096
  10.2 0.0 copy-done.2
  10.2 3.1 %keys_values.1 = (bf16[128,256]{1,0:T(8,128)(2,1)}, bf16[128,2048]{1,0:T(8,128)(2,1)}) custom-call(s32[2]{0:T(128)} %pad_add_fusion.place, bf16[128,512]{1,0:T(8,128)(2,1)} %x0.1, bf16[128,512]{1,0:T(8,128)(2,1)} %copy-done, bf16[128,512]{1,0:T(8,128)(2,1)} %copy-done.1, bf16[128,512]{1,0:T(8,128)(2,1)} %copy-done.2, f32[1,2048]{1,0:T(1,128)} %bitcast.7, ...), custom_call_target="tpu_custom_call" | custom-call | tf_op jit(solution)/shard_map/keys_values/pallas_call | solution.py:315
  13.3 1.8 %collective-permute-start.3 = (bf16[128,256]{1,0:T(8,128)(2,1)}, bf16[128,256]{1,0:T(8,128)(2,1)S(1)}, u32[]{:S(2)}, u32[]{:S(2)}) collective-permute-start(bf16[128,256]{1,0:T(8,128)(2,1)} %get-tuple-element.8.refs_0_), channel_id=1, source_target_pairs={{0,8},{1,5},{2,10},{3,7},{4,12},{5,1},{6,14},{7,3},{8,0},{9,13},{1... | collective-permute-start | bytes 196616 | tf_op jit(solution)/shard_map/ppermute | solution.py:301
  15.1 2.6 %collective-permute-start.6 = (bf16[128,256]{1,0:T(8,128)(2,1)}, bf16[128,256]{1,0:T(8,128)(2,1)S(1)}, u32[]{:S(2)}, u32[]{:S(2)}) collective-permute-start(bf16[128,256]{1,0:T(8,128)(2,1)} %get-tuple-element.8.refs_0_), channel_id=1, source_target_pairs={{0,16},{1,25},{2,18},{3,27},{4,20},{5,29},{6,22},{7,31},{8,24},{9,... | collective-permute-start | bytes 196616 | tf_op jit(solution)/shard_map/ppermute | solution.py:301
  17.7 1.3 %collective-permute-start.8 = (bf16[128,256]{1,0:T(8,128)(2,1)}, bf16[128,256]{1,0:T(8,128)(2,1)S(1)}, u32[]{:S(2)}, u32[]{:S(2)}) collective-permute-start(bf16[128,256]{1,0:T(8,128)(2,1)} %get-tuple-element.8.refs_0_), channel_id=1, source_target_pairs={{0,20},{1,29},{2,22},{3,31},{4,16},{5,25},{6,18},{7,27},{8,28},{9,... | collective-permute-start | bytes 196616 | tf_op jit(solution)/shard_map/ppermute | solution.py:301
  19.0 0.0 collective-permute-done.3
  19.0 0.0 collective-permute-start.4
  19.0 0.0 copy-done.4
  19.0 0.7 %copy.18.caption = s32[128,1]{1,0:T(8,128)} copy(s32[128,1]{0,1:T(1,128)S(1)} %bitcast.8) | data formatting | bytes 1024 | tf_op jit(solution)/shard_map/broadcast_in_dim | solution.py:372
  19.7 1.5 %collective-permute-start.5 = (bf16[128,256]{1,0:T(8,128)(2,1)}, bf16[128,256]{1,0:T(8,128)(2,1)S(1)}, u32[]{:S(2)}, u32[]{:S(2)}) collective-permute-start(bf16[128,256]{1,0:T(8,128)(2,1)} %get-tuple-element.8.refs_0_), channel_id=1, source_target_pairs={{0,12},{1,13},{2,14},{3,15},{4,8},{5,9},{6,10},{7,11},{8,4},{9,5},... | collective-permute-start | bytes 196616 | tf_op jit(solution)/shard_map/ppermute | solution.py:301
  21.3 2.9 %queries.1.q = bf16[128,512]{1,0:T(8,128)(2,1)} custom-call(bf16[128,2048]{1,0:T(8,128)(2,1)} %get-tuple-element.7.normed, bf16[2048,512]{1,0:T(8,128)(2,1)} %weight.1, f32[128,128]{1,0:T(8,128)} %copy.16.cosine, f32[128,128]{1,0:T(8,128)} %pad_maximum_fusion.sine), custom_call_target="tpu_custom_call" | custom-call | tf_op jit(solution)/shard_map/queries/pallas_call | solution.py:344
  24.2 0.0 collective-permute-done.6
  24.2 0.2 collective-permute-start.7
  24.4 1.0 %collective-permute-done.8 = bf16[128,256]{1,0:T(8,128)(2,1)S(1)} collective-permute-done((bf16[128,256]{1,0:T(8,128)(2,1)}, bf16[128,256]{1,0:T(8,128)(2,1)S(1)}, u32[]{:S(2)}, u32[]{:S(2)}) %collective-permute-start.8) | collective-permute-done | bytes 65568 | tf_op jit(solution)/shard_map/ppermute | solution.py:301
  25.4 0.0 collective-permute-start.9
  25.4 0.0 collective-permute-done.4
  25.4 0.7 %broadcast_select_fusion.4 = (bf16[128,256]{1,0:T(8,128)(2,1)}, bf16[128,256]{1,0:T(8,128)(2,1)}) fusion(bf16[128,256]{1,0:T(8,128)(2,1)S(1)} %collective-permute-done.4, bf16[128,256]{1,0:T(8,128)(2,1)S(1)} %collective-permute-done.3, pred[]{:T(512)S(6)} %eq.5), kind=kLoop, calls=%fused_computation.7 | loop fusion | flops 65536 | bytes 262145 | tf_op jit(solution)/shard_map/jit(_where)/select_n | solution.py:355
  26.1 0.0 collective-permute-done.7
  26.1 0.7 %broadcast_select_fusion.1 = (bf16[128,256]{1,0:T(8,128)(2,1)}, bf16[128,256]{1,0:T(8,128)(2,1)}) fusion(bf16[128,256]{1,0:T(8,128)(2,1)S(1)} %collective-permute-done.6, bf16[128,256]{1,0:T(8,128)(2,1)S(1)} %collective-permute-done.7, pred[]{:T(512)S(6)} %eq.5), kind=kLoop, calls=%fused_computation.4 | loop fusion | flops 65536 | bytes 262145 | tf_op jit(solution)/shard_map/jit(_where)/select_n | solution.py:356
  26.7 0.0 collective-permute-done.9
  26.7 0.7 %broadcast_select_fusion = (bf16[128,256]{1,0:T(8,128)(2,1)}, bf16[128,256]{1,0:T(8,128)(2,1)}) fusion(bf16[128,256]{1,0:T(8,128)(2,1)S(1)} %collective-permute-done.8, bf16[128,256]{1,0:T(8,128)(2,1)S(1)} %collective-permute-done.9, pred[]{:T(512)S(6)} %eq.5), kind=kLoop, calls=%fused_computation.3 | loop fusion | flops 65536 | bytes 262145 | tf_op jit(solution)/shard_map/jit(_where)/select_n | solution.py:356
  27.4 0.0 collective-permute-done.5.refs_3_
  27.4 0.0 copy-start.3
  27.4 0.6 %copy-done.3 = bf16[128,256]{1,0:T(8,128)(2,1)} copy-done((bf16[128,256]{1,0:T(8,128)(2,1)}, bf16[128,256]{1,0:T(8,128)(2,1)S(1)}, u32[]{:S(2)}) %copy-start.3) | copy-done | bytes 65560
  28.0 4.0 %attend.1 = bf16[128,512]{1,0:T(8,128)(2,1)} custom-call(s32[1]{0:T(128)} %bitcast.place, s32[8]{0:T(128)} %lengths.1, s32[1,2]{1,0:T(1,128)} %spans.1, bf16[128,512]{1,0:T(8,128)(2,1)} %queries.1.q, s32[128,1]{1,0:T(8,128)} %copy.18.caption, bf16[128,256]{1,0:T(8,128)(2,1)} %get-tuple-element.8.refs_0_, bf16[128,256]{1,0:T(8,128)(2,1)} %get-tuple-element.14.refs_1_, ...), custom_call_target="tpu_custom_call" | custom-call | tf_op jit(solution)/shard_map/attend/pallas_call | solution.py:357
  (3 shorter events, 0.0 us)
Async XLA Ops:
  0.0 19.0 %copy-start.4 = (s32[128]{0:T(128)S(1)}, s32[128]{0:T(128)}, u32[]{:S(2)}) copy-start(s32[128]{0:T(128)} %param.14) | copy-start | bytes 1540
  0.0 9.5 %collective-permute-start = (bf16[128,512]{1,0:T(8,128)(2,1)}, bf16[128,512]{1,0:T(8,128)(2,1)S(1)}, u32[]{:S(2)}, u32[]{:S(2)}) collective-permute-start(bf16[128,512]{1,0:T(8,128)(2,1)} %x0.1), channel_id=1, source_target_pairs={{0,1},{1,0},{2,3},{3,2},{4,5},{5,4},{6,7},{7,6},{8,9},{9,8},{10,11... | collective-permute-start | bytes 393224 | tf_op jit(solution)/shard_map/ppermute | solution.py:301
  0.5 6.9 %collective-permute-start.1 = (bf16[128,512]{1,0:T(8,128)(2,1)}, bf16[128,512]{1,0:T(8,128)(2,1)S(1)}, u32[]{:S(2)}, u32[]{:S(2)}) collective-permute-start(bf16[128,512]{1,0:T(8,128)(2,1)} %x0.1), channel_id=1, source_target_pairs={{0,2},{1,3},{2,0},{3,1},{4,6},{5,7},{6,4},{7,5},{8,10},{9,11},{10,... | collective-permute-start | bytes 393224 | tf_op jit(solution)/shard_map/ppermute | solution.py:301
  7.4 2.2 %copy-start.1 = (bf16[128,512]{1,0:T(8,128)(2,1)}, bf16[128,512]{1,0:T(8,128)(2,1)S(1)}, u32[]{:S(2)}) copy-start(bf16[128,512]{1,0:T(8,128)(2,1)S(1)} %collective-permute-done.1.x2) | copy-start | bytes 393220
  7.4 2.2 %collective-permute-start.2 = (bf16[128,512]{1,0:T(8,128)(2,1)S(1)}, bf16[128,512]{1,0:T(8,128)(2,1)S(1)}, u32[]{:S(2)}, u32[]{:S(2)}) collective-permute-start(bf16[128,512]{1,0:T(8,128)(2,1)S(1)} %collective-permute-done.1.x2), channel_id=1, source_target_pairs={{0,1},{1,0},{2,3},{3,2},{4,5},{5,4},{6,7},{7,6},{8,9},{9,8},{10,11... | collective-permute-start | bytes 393224 | tf_op jit(solution)/shard_map/ppermute | solution.py:301
  9.6 0.7 %copy-start = (bf16[128,512]{1,0:T(8,128)(2,1)}, bf16[128,512]{1,0:T(8,128)(2,1)S(1)}, u32[]{:S(2)}) copy-start(bf16[128,512]{1,0:T(8,128)(2,1)S(1)} %collective-permute-done.x1) | copy-start | bytes 393220
  9.6 0.7 %copy-start.2 = (bf16[128,512]{1,0:T(8,128)(2,1)}, bf16[128,512]{1,0:T(8,128)(2,1)S(1)}, u32[]{:S(2)}) copy-start(bf16[128,512]{1,0:T(8,128)(2,1)S(1)} %collective-permute-done.2.x3) | copy-start | bytes 393220
  13.3 5.7 %collective-permute-start.3 = (bf16[128,256]{1,0:T(8,128)(2,1)}, bf16[128,256]{1,0:T(8,128)(2,1)S(1)}, u32[]{:S(2)}, u32[]{:S(2)}) collective-permute-start(bf16[128,256]{1,0:T(8,128)(2,1)} %get-tuple-element.8.refs_0_), channel_id=1, source_target_pairs={{0,8},{1,5},{2,10},{3,7},{4,12},{5,1},{6,14},{7,3},{8,0},{9,13},{1... | collective-permute-start | bytes 196616 | tf_op jit(solution)/shard_map/ppermute | solution.py:301
  15.1 9.0 %collective-permute-start.6 = (bf16[128,256]{1,0:T(8,128)(2,1)}, bf16[128,256]{1,0:T(8,128)(2,1)S(1)}, u32[]{:S(2)}, u32[]{:S(2)}) collective-permute-start(bf16[128,256]{1,0:T(8,128)(2,1)} %get-tuple-element.8.refs_0_), channel_id=1, source_target_pairs={{0,16},{1,25},{2,18},{3,27},{4,20},{5,29},{6,22},{7,31},{8,24},{9,... | collective-permute-start | bytes 196616 | tf_op jit(solution)/shard_map/ppermute | solution.py:301
  17.7 7.7 %collective-permute-start.8 = (bf16[128,256]{1,0:T(8,128)(2,1)}, bf16[128,256]{1,0:T(8,128)(2,1)S(1)}, u32[]{:S(2)}, u32[]{:S(2)}) collective-permute-start(bf16[128,256]{1,0:T(8,128)(2,1)} %get-tuple-element.8.refs_0_), channel_id=1, source_target_pairs={{0,20},{1,29},{2,22},{3,31},{4,16},{5,25},{6,18},{7,27},{8,28},{9,... | collective-permute-start | bytes 196616 | tf_op jit(solution)/shard_map/ppermute | solution.py:301
  19.0 6.4 %collective-permute-start.4 = (bf16[128,256]{1,0:T(8,128)(2,1)S(1)}, bf16[128,256]{1,0:T(8,128)(2,1)S(1)}, u32[]{:S(2)}, u32[]{:S(2)}) collective-permute-start(bf16[128,256]{1,0:T(8,128)(2,1)S(1)} %collective-permute-done.3), channel_id=1, source_target_pairs={{0,1},{1,0},{2,3},{3,2},{4,5},{5,4},{6,7},{7,6},{8,9},{9,8},{10,11... | collective-permute-start | bytes 196616 | tf_op jit(solution)/shard_map/ppermute | solution.py:301
  19.7 7.7 %collective-permute-start.5 = (bf16[128,256]{1,0:T(8,128)(2,1)}, bf16[128,256]{1,0:T(8,128)(2,1)S(1)}, u32[]{:S(2)}, u32[]{:S(2)}) collective-permute-start(bf16[128,256]{1,0:T(8,128)(2,1)} %get-tuple-element.8.refs_0_), channel_id=1, source_target_pairs={{0,12},{1,13},{2,14},{3,15},{4,8},{5,9},{6,10},{7,11},{8,4},{9,5},... | collective-permute-start | bytes 196616 | tf_op jit(solution)/shard_map/ppermute | solution.py:301
  24.2 1.9 %collective-permute-start.7 = (bf16[128,256]{1,0:T(8,128)(2,1)S(1)}, bf16[128,256]{1,0:T(8,128)(2,1)S(1)}, u32[]{:S(2)}, u32[]{:S(2)}) collective-permute-start(bf16[128,256]{1,0:T(8,128)(2,1)S(1)} %collective-permute-done.6), channel_id=1, source_target_pairs={{0,1},{1,0},{2,3},{3,2},{4,5},{5,4},{6,7},{7,6},{8,9},{9,8},{10,11... | collective-permute-start | bytes 196616 | tf_op jit(solution)/shard_map/ppermute | solution.py:301
  25.4 1.4 %collective-permute-start.9 = (bf16[128,256]{1,0:T(8,128)(2,1)S(1)}, bf16[128,256]{1,0:T(8,128)(2,1)S(1)}, u32[]{:S(2)}, u32[]{:S(2)}) collective-permute-start(bf16[128,256]{1,0:T(8,128)(2,1)S(1)} %collective-permute-done.8), channel_id=1, source_target_pairs={{0,1},{1,0},{2,3},{3,2},{4,5},{5,4},{6,7},{7,6},{8,9},{9,8},{10,11... | collective-permute-start | bytes 196616 | tf_op jit(solution)/shard_map/ppermute | solution.py:301
  27.4 0.6 %copy-start.3 = (bf16[128,256]{1,0:T(8,128)(2,1)}, bf16[128,256]{1,0:T(8,128)(2,1)S(1)}, u32[]{:S(2)}) copy-start(bf16[128,256]{1,0:T(8,128)(2,1)S(1)} %collective-permute-done.5.refs_3_) | copy-start | bytes 196612

commit v2 on v1

--- a/solution.py
+++ b/solution.py
@@ -185,51 +185,77 @@
     return [pl.BlockSpec(memory_space=pltpu.SMEM)] * count
 
 
+def grant(mebibytes):
+    return pltpu.CompilerParams(vmem_limit_bytes=mebibytes << 20)
+
+
+def near_core(array):
+    return pltpu.with_memory_space_constraint(array, pltpu.VMEM)
+
+
 def turn(u, cosine, sine):
     return u * cosine + pltpu.roll(u, u.shape[-1] // 2, 1) * sine
 
 
-def kv_kernel(
-    place, x0, x1, x2, x3, gain, key_weight, value_weight, cosine, sine, kv_out, normed_out
-):
+def tables(cosine, sine):
+    c, s = cosine[...], sine[...]
+    return jnp.concatenate([c, c], 1), jnp.concatenate([-s, s], 1)
+
+
+def load_kernel(sharers, tokens, gain, key_weight, value_weight, query_weight, caption, *refs):
+    outs, sems = refs[:-1], refs[-1]
+    tokens_out, gain_out, weight_out, query_out, caption_out = outs
+    column = pl.multiple_of(lax.axis_index("head") // sharers * HD, HD)
+    pairs = (
+        (key_weight.at[:, pl.ds(column, HD)], weight_out.at[:, :HD]),
+        (value_weight.at[:, pl.ds(column, HD)], weight_out.at[:, HD:]),
+        (tokens, tokens_out),
+        (gain, gain_out),
+        (caption, caption_out),
+        (query_weight, query_out),
+    )
+    copies = [pltpu.make_async_copy(a, b, sems.at[i]) for i, (a, b) in enumerate(pairs)]
+    for copy in copies:
+        copy.start()
+    for copy in copies:
+        copy.wait()
+
+
+def kv_kernel(x0, x1, x2, x3, gain, weight, cosine, sine, kv_out, normed_out):
     depth = x0.shape[1]
     parts = (x0, x1, x2, x3)
-    me, kv_col = place[0], pl.multiple_of(place[1], HD)
+    me = lax.axis_index("head")
     total = None
     for part in parts:
         hidden = part[...].astype(jnp.float32)
         squares = jnp.sum(hidden * hidden, -1, keepdims=True)
         total = squares if total is None else total + squares
     scale = lax.rsqrt(total / (depth * len(parts)) + norm_eps)
-    keys = values = None
+    both = None
     for order, part in enumerate(parts):
         first = pl.multiple_of(jnp.bitwise_xor(me, order) * depth, depth)
         span = pl.ds(first, depth)
         normed = (part[...].astype(jnp.float32) * scale * gain[:, span]).astype(jnp.bfloat16)
         normed_out[:, span] = normed
-        k = jnp.dot(
-            normed, key_weight[span, pl.ds(kv_col, HD)], preferred_element_type=jnp.float32
-        )
-        v = jnp.dot(
-            normed, value_weight[span, pl.ds(kv_col, HD)], preferred_element_type=jnp.float32
-        )
-        keys = k if keys is None else keys + k
-        values = v if values is None else values + v
-    kv_out[:, :HD] = turn(keys, cosine[...], sine[...]).astype(jnp.bfloat16)
-    kv_out[:, HD:] = values.astype(jnp.bfloat16)
+        product = jnp.dot(normed, weight[span, :], preferred_element_type=jnp.float32)
+        both = product if both is None else both + product
+    kv_out[:, :HD] = turn(both[:, :HD], *tables(cosine, sine)).astype(jnp.bfloat16)
+    kv_out[:, HD:] = both[:, HD:].astype(jnp.bfloat16)
 
 
 def query_kernel(normed, weight, cosine, sine, out):
     q = jnp.dot(normed[...], weight[...], preferred_element_type=jnp.float32)
+    c, s = tables(cosine, sine)
     for begin in range(0, q.shape[1], HD):
-        turned = turn(q[:, begin : begin + HD], cosine[...], sine[...])
+        turned = turn(q[:, begin : begin + HD], c, s)
         out[:, begin : begin + HD] = (turned * HD ** (-0.5)).astype(jnp.bfloat16)
 
 
-def attend_kernel(blocks, place, lengths, spans, q, caption, *refs):
+def attend_kernel(offsets, lengths, spans, q, caption, *refs):
+    blocks = len(offsets)
     kv, (out, scores, bias) = refs[:blocks], refs[blocks:]
     rows = q.shape[0]
-    rank = place[0]
+    rank, odd = lax.axis_index("seq"), lax.rem(lax.axis_index("head"), 2)
     row_pos = rank * rows + lax.broadcasted_iota(jnp.int32, (rows, BLOCK), 0)
     first_row = jnp.zeros((rows, BLOCK), jnp.int32)
     begin = jnp.int32(0)
@@ -238,9 +264,10 @@
         within = (row_pos >= begin) & (row_pos < end)
         first_row = jnp.where(within, begin, first_row)
         begin = end
-    is_caption = jnp.broadcast_to(caption[...], (rows, BLOCK)) == 1
-    for order in range(blocks):
-        block = jnp.bitwise_xor(rank, order)
+    is_caption = jnp.broadcast_to(caption[...], (rows, rows)).T == 1
+    for order, (even_offset, odd_offset) in enumerate(offsets):
+        offset = even_offset + odd * (odd_offset - even_offset)
+        block = jnp.bitwise_xor(rank, offset)
         key_pos = block * BLOCK + lax.broadcasted_iota(jnp.int32, (rows, BLOCK), 1)
         near = (first_row <= key_pos) & (key_pos <= row_pos)
         reached = (spans[0, 0] <= block) & (block <= spans[0, 1])
@@ -286,91 +313,109 @@
     span_blocks,
 ):
     ranks, groups = lax.axis_size("seq"), lax.axis_size("head")
-    rank, group = lax.axis_index("seq"), lax.axis_index("head")
+    rank = lax.axis_index("seq")
     rows = tokens.shape[0]
     head_dev = query_weight.shape[1] // HD
 
-    def pairs(shift):
-        return [
+    def move(array, shift):
+        pairs = [
             (r * groups + g, (r ^ shift(g)[0]) * groups + (g ^ shift(g)[1]))
             for r in range(ranks)
             for g in range(groups)
         ]
-
-    def move(array, shift):
-        return lax.ppermute(array, ("seq", "head"), pairs(shift))
+        return lax.ppermute(array, ("seq", "head"), pairs)
 
     across = move(tokens, lambda g: (0, 2))
     beside = move(tokens, lambda g: (0, 1))
+    features = query_weight.shape[0]
+    row, gain, kv_weight, wide, captions = pl.pallas_call(
+        functools.partial(load_kernel, H // KV // head_dev),
+        out_shape=(
+            pltpu.VMEM(tokens.shape, tokens.dtype),
+            pltpu.VMEM((1, features), norm_gain.dtype),
+            pltpu.VMEM((features, 2 * HD), key_weight.dtype),
+            pltpu.VMEM(query_weight.shape, query_weight.dtype),
+            pltpu.VMEM((1, rows), is_caption.dtype),
+        ),
+        in_specs=[pl.BlockSpec(memory_space=pltpu.HBM)] * 6,
+        out_specs=tuple(vmem(5)),
+        scratch_shapes=[pltpu.SemaphoreType.DMA((6,))],
+        compiler_params=grant(2),
+        name="load",
+    )(
+        *[
+            pltpu.with_memory_space_constraint(array, pltpu.HBM)
+            for array in (
+                tokens,
+                norm_gain[None, :],
+                key_weight,
+                value_weight,
+                query_weight,
+                is_caption[None, :],
+            )
+        ]
+    )
     half = HD // 2
     frequency = rope_base ** (-jnp.arange(half, dtype=jnp.float32) * 2.0 / HD)
     row_pos = rank * rows + jnp.arange(rows, dtype=jnp.int32)
     angles = row_pos.astype(jnp.float32)[:, None] * frequency[None, :]
-    cosine = jnp.tile(jnp.cos(angles), (1, 2))
-    sine = jnp.sin(angles)
-    sine = jnp.concatenate([-sine, sine], 1)
+    cosine, sine = near_core(jnp.cos(angles)), near_core(jnp.sin(angles))
     corner = move(across, lambda g: (0, 1))
 
-    kv_index = group * head_dev // (H // KV)
     key_values, normed = pl.pallas_call(
         kv_kernel,
         out_shape=(
-            jax.ShapeDtypeStruct((rows, 2 * HD), jnp.bfloat16),
-            jax.ShapeDtypeStruct((rows, query_weight.shape[0]), jnp.bfloat16),
+            pltpu.VMEM((rows, 2 * HD), jnp.bfloat16),
+            pltpu.VMEM((rows, features), jnp.bfloat16),
         ),
-        in_specs=smem(1) + vmem(9),
+        in_specs=vmem(8),
         out_specs=tuple(vmem(2)),
+        compiler_params=grant(6),
         name="keys_values",
     )(
-        jnp.stack([group, kv_index * HD]),
-        tokens,
-        beside,
-        across,
-        corner,
-        norm_gain[None, :],
-        key_weight,
-        value_weight,
+        near_core(row),
+        near_core(beside),
+        near_core(across),
+        near_core(corner),
+        near_core(gain),
+        near_core(kv_weight),
         cosine,
         sine,
     )
 
-    blocks = {0: key_values}
     far = ranks // 2
     plan = [(far, far | 2), (far | 1, far | 3), (2, 1)]
-    fetched = [
-        (both, move(key_values, lambda g, both=both: (both[g % 2], 0))) for both in plan
-    ]
+    fetched = [move(key_values, lambda g, both=both: (both[g % 2], 0)) for both in plan]
     last = move(key_values, lambda g: (3, 0))
     queries = pl.pallas_call(
         query_kernel,
-        out_shape=jax.ShapeDtypeStruct((rows, head_dev * HD), jnp.bfloat16),
+        out_shape=pltpu.VMEM((rows, head_dev * HD), jnp.bfloat16),
         in_specs=vmem(4),
         out_specs=vmem(1)[0],
+        compiler_params=grant(4),
         name="queries",
-    )(normed, query_weight, cosine, sine)
-    odd = group % 2 == 1
-    held = {0: key_values, 3: last}
-    for both, own in fetched:
-        other = move(own, lambda g: (0, 1))
-        held[both[0]] = jnp.where(odd, other, own)
-        held[both[1]] = jnp.where(odd, own, other)
+    )(near_core(normed), near_core(wide), cosine, sine)
+    offsets, held = [(0, 0), (3, 3)], [key_values, last]
+    for both, own in zip(plan, fetched):
+        offsets += [both, both[::-1]]
+        held += [own, move(own, lambda g: (0, 1))]
     return pl.pallas_call(
-        functools.partial(attend_kernel, ranks),
+        functools.partial(attend_kernel, offsets),
         out_shape=jax.ShapeDtypeStruct((rows, head_dev * HD), jnp.bfloat16),
-        in_specs=smem(3) + vmem(2 + ranks),
+        in_specs=smem(2) + vmem(2 + ranks),
         out_specs=vmem(1)[0],
         scratch_shapes=[
             pltpu.VMEM((rows, ranks * BLOCK), jnp.float32),
             pltpu.VMEM((rows, ranks * BLOCK), jnp.float32),
         ],
+        compiler_params=grant(8),
         name="attend",
     )(
-        rank[None],
         window_lengths,
         span_blocks,
-        queries,
-        is_caption[:, None],
-        *[held[order] for order in range(ranks)],
+        near_core(queries),
+        near_core(captions),
+        *[near_core(array) for array in held],
     )
 
 

time: 32.2 us -> 24.9 us (0.77)
  waiting for transfers between devices: 4.99 us -> 8.81 us
  other arithmetic: 3.69 us -> 0.32 us
  Pallas kernels: 9.93 us -> 6.69 us
  local copies, waits for them, and re-layouts: 2.85 us -> 0.01 us
  starting transfers between devices: 10.5 us -> 8.92 us
    ppermute x10, waiting for transfers between devices: 4.99 us -> 8.81 us  [move(): return lax.ppermute(array, ('seq', 'head'), pairs)]
    pallas_call x3 -> x4, Pallas kernels: 9.93 us -> 6.69 us  [the longest x1 3.46 us: everywhere(): pl.pallas_call(functools.partial(attend_kernel, offsets), out_shape=jax.S...]
    select_n x3 -> x0, other arithmetic: 2.01 us -> none  [the longest x2 1.33 us: everywhere(): held[both[1]] = jnp.where(odd, own, other)]
    ppermute x10, starting transfers between devices: 10.5 us -> 8.92 us  [move(): return lax.ppermute(array, ('seq', 'head'), pairs)]
    unnamed x10 -> x4, local copies, waits for them, and re-layouts: 1.3 us -> 0.01 us
    broadcast_in_dim x1 -> x0, local copies, waits for them, and re-layouts: 0.75 us -> none  [everywhere(): is_caption[:, None]]
    another operation x2 -> x0, local copies, waits for them, and re-layouts: 0.74 us -> none  [everywhere(): cosine = jnp.tile(jnp.cos(angles), (1, 2))]
    concatenate x1 -> x0, other arithmetic: 0.7 us -> none  [everywhere(): sine = jnp.concatenate([-sine, sine], 1)]
  transfers between devices with their start and end apart: 10 -> 10, of which waited for: 2 -> 6; matrix products, arithmetic and copies ran while one was open for 16% -> 1% of each run, Pallas kernels for 9% -> 11%
where the time goes in v2:
time: 24.9 us; the launch traced here: 24.8 us
  starting transfers between devices  8.92 us (36%)
  waiting for transfers between devices  8.81 us (35%)
  Pallas kernels  6.69 us (27%)
  other arithmetic  0.32 us (1%)
    ppermute x10, starting transfers between devices, move(): return lax.ppermute(array, ('seq', 'head'), pairs)  8.92 us
    ppermute x10, waiting for transfers between devices, move(): return lax.ppermute(array, ('seq', 'head'), pairs)  8.81 us
    pallas_call x1, Pallas kernels, everywhere(): pl.pallas_call(functools.partial(attend_kernel, offsets), out_shape=jax.S...  3.46 us
    pallas_call x1, Pallas kernels, everywhere(): pl.pallas_call(functools.partial(load_kernel, H // KV // head_dev), out_s...  2.07 us
    pallas_call x1, Pallas kernels, everywhere(): pl.pallas_call(query_kernel, out_shape=pltpu.VMEM((rows, head_dev * HD),...  0.58 us
    pallas_call x1, Pallas kernels, everywhere(): pl.pallas_call(kv_kernel, out_shape=(pltpu.VMEM((rows, 2 * HD), jnp.bfloa...  0.58 us
  transfers between devices with their start and end apart: 10, of which 6 were waited for; matrix products, arithmetic and copies ran while one was open for 1% of the time, Pallas kernels for 11%

profile of v2, /device:TPU:0, one launch (start us, length us, event | category | flops | bytes accessed | tf_op | source)
XLA Modules:
  0.0 24.8 jit_solution(14665768521291466908)
XLA Ops:
  0.0 3.0 %collective-permute-start.1 = (bf16[128,512]{1,0:T(8,128)(2,1)}, bf16[128,512]{1,0:T(8,128)(2,1)S(1)}, u32[]{:S(2)}, u32[]{:S(2)}) collective-permute-start(bf16[128,512]{1,0:T(8,128)(2,1)} %tokens.1), channel_id=1, source_target_pairs={{0,2},{1,3},{2,0},{3,1},{4,6},{5,7},{6,4},{7,5},{8,10},{9,11},{10,... | collective-permute-start | bytes 393224 | tf_op jit(solution)/shard_map/ppermute | solution.py:326
  3.0 0.0 collective-permute-start
  3.0 2.1 %load.1 = (bf16[128,512]{1,0:T(8,128)(2,1)S(1)}, f32[1,2048]{1,0:T(1,128)S(1)}, bf16[2048,256]{1,0:T(8,128)(2,1)S(1)}, bf16[2048,512]{1,0:T(8,128)(2,1)S(1)}, s32[1,128]{1,0:T(1,128)S(1)}) custom-call(bf16[128,512]{1,0:T(8,128)(2,1)} %tokens.1, f32[1,2048]{1,0:T(1,128)} %bitcast.2, bf16[2048,256]{1,0:T(8,128)(2,1)} %key_weight.1, ...), custom_call_target="tpu_custom_call" | custom-call | tf_op jit(solution)/shard_map/load/pallas_call | solution.py:331
  5.1 1.6 %collective-permute-done.1.x2 = bf16[128,512]{1,0:T(8,128)(2,1)S(1)} collective-permute-done((bf16[128,512]{1,0:T(8,128)(2,1)}, bf16[128,512]{1,0:T(8,128)(2,1)S(1)}, u32[]{:S(2)}, u32[]{:S(2)}) %collective-permute-start.1) | collective-permute-done | bytes 131104 | tf_op jit(solution)/shard_map/ppermute | solution.py:326
  6.7 0.0 collective-permute-start.2
  6.7 0.3 %multiply_sine_fusion = (f32[128,64]{1,0:T(8,128)S(1)}, f32[128,64]{1,0:T(8,128)S(1)}) fusion(f32[64]{0:T(128)S(1)} %multiply_power_fusion, f32[128]{0:T(128)S(1)} %add_convert_fusion), kind=kLoop, calls=%fused_computation | loop fusion | flops 8192 | bytes 66304 | tf_op jit(solution)/shard_map/sin | solution.py:362
  7.0 0.0 collective-permute-done.x1
  7.0 1.0 %collective-permute-done.2.x3 = bf16[128,512]{1,0:T(8,128)(2,1)S(1)} collective-permute-done((bf16[128,512]{1,0:T(8,128)(2,1)S(1)}, bf16[128,512]{1,0:T(8,128)(2,1)S(1)}, u32[]{:S(2)}, u32[]{:S(2)}) %collective-permute-start.2) | collective-permute-done | bytes 131104 | tf_op jit(solution)/shard_map/ppermute | solution.py:326
  8.0 0.0 copy-start
  8.1 0.0 copy-start.1
  8.1 0.6 %keys_values.1 = (bf16[128,256]{1,0:T(8,128)(2,1)S(1)}, bf16[128,2048]{1,0:T(8,128)(2,1)S(1)}) custom-call(bf16[128,512]{1,0:T(8,128)(2,1)S(1)} %get-tuple-element.12.x0, bf16[128,512]{1,0:T(8,128)(2,1)S(1)} %collective-permute-done.x1, bf16[128,512]{1,0:T(8,128)(2,1)S(1)} %collective-permute-done.1.x2, bf16[128,512]{1,0:T(8,128)(2,1)S(1)} %collective-permute-done.2.x3, ...), custom_call_target="tpu_custom_call" | custom-call | tf_op jit(solution)/shard_map/keys_values/pallas_call | solution.py:365
  8.6 1.9 %collective-permute-start.8 = (bf16[128,256]{1,0:T(8,128)(2,1)S(1)}, bf16[128,256]{1,0:T(8,128)(2,1)S(1)}, u32[]{:S(2)}, u32[]{:S(2)}) collective-permute-start(bf16[128,256]{1,0:T(8,128)(2,1)S(1)} %get-tuple-element.18.refs_0_), channel_id=1, source_target_pairs={{0,8},{1,5},{2,10},{3,7},{4,12},{5,1},{6,14},{7,3},{8,0},{9,13},{1... | collective-permute-start | bytes 196616 | tf_op jit(solution)/shard_map/ppermute | solution.py:326
  10.5 3.5 %collective-permute-start.6 = (bf16[128,256]{1,0:T(8,128)(2,1)S(1)}, bf16[128,256]{1,0:T(8,128)(2,1)S(1)}, u32[]{:S(2)}, u32[]{:S(2)}) collective-permute-start(bf16[128,256]{1,0:T(8,128)(2,1)S(1)} %get-tuple-element.18.refs_0_), channel_id=1, source_target_pairs={{0,20},{1,29},{2,22},{3,31},{4,16},{5,25},{6,18},{7,27},{8,28},{9,... | collective-permute-start | bytes 196616 | tf_op jit(solution)/shard_map/ppermute | solution.py:326
  14.0 0.3 %collective-permute-start.4 = (bf16[128,256]{1,0:T(8,128)(2,1)S(1)}, bf16[128,256]{1,0:T(8,128)(2,1)S(1)}, u32[]{:S(2)}, u32[]{:S(2)}) collective-permute-start(bf16[128,256]{1,0:T(8,128)(2,1)S(1)} %get-tuple-element.18.refs_0_), channel_id=1, source_target_pairs={{0,16},{1,25},{2,18},{3,27},{4,20},{5,29},{6,22},{7,31},{8,24},{9,... | collective-permute-start | bytes 196616 | tf_op jit(solution)/shard_map/ppermute | solution.py:326
  14.4 0.2 collective-permute-start.3
  14.6 0.0 collective-permute-done.8.refs_6_
  14.6 0.0 collective-permute-start.9
  14.6 3.9 %collective-permute-done.6.refs_4_ = bf16[128,256]{1,0:T(8,128)(2,1)S(1)} collective-permute-done((bf16[128,256]{1,0:T(8,128)(2,1)S(1)}, bf16[128,256]{1,0:T(8,128)(2,1)S(1)}, u32[]{:S(2)}, u32[]{:S(2)}) %collective-permute-start.6) | collective-permute-done | bytes 65568 | tf_op jit(solution)/shard_map/ppermute | solution.py:326
  18.4 0.0 collective-permute-start.7
  18.4 1.7 %collective-permute-done.4.refs_2_ = bf16[128,256]{1,0:T(8,128)(2,1)S(1)} collective-permute-done((bf16[128,256]{1,0:T(8,128)(2,1)S(1)}, bf16[128,256]{1,0:T(8,128)(2,1)S(1)}, u32[]{:S(2)}, u32[]{:S(2)}) %collective-permute-start.4) | collective-permute-done | bytes 65568 | tf_op jit(solution)/shard_map/ppermute | solution.py:326
  20.1 0.0 collective-permute-start.5
  20.1 0.6 %queries.1.q = bf16[128,512]{1,0:T(8,128)(2,1)S(1)} custom-call(bf16[128,2048]{1,0:T(8,128)(2,1)S(1)} %get-tuple-element.15.normed, bf16[2048,512]{1,0:T(8,128)(2,1)S(1)} %get-tuple-element.16.weight, f32[128,64]{1,0:T(8,128)S(1)} %get-tuple-element.20.cosine, f32[128,64]{1,0:T(8,128)S(1)} %get-tuple-element.19.sine), custom_call_target="tpu_custom_call" | custom-call | tf_op jit(solution)/shard_map/queries/pallas_call | solution.py:390
  20.7 0.3 %collective-permute-done.3.refs_1_ = bf16[128,256]{1,0:T(8,128)(2,1)S(1)} collective-permute-done((bf16[128,256]{1,0:T(8,128)(2,1)S(1)}, bf16[128,256]{1,0:T(8,128)(2,1)S(1)}, u32[]{:S(2)}, u32[]{:S(2)}) %collective-permute-start.3) | collective-permute-done | bytes 65568 | tf_op jit(solution)/shard_map/ppermute | solution.py:326
  20.9 0.0 collective-permute-done.9.refs_7_
  20.9 0.0 collective-permute-done.7.refs_5_
  20.9 0.4 %collective-permute-done.5.refs_3_ = bf16[128,256]{1,0:T(8,128)(2,1)S(1)} collective-permute-done((bf16[128,256]{1,0:T(8,128)(2,1)S(1)}, bf16[128,256]{1,0:T(8,128)(2,1)S(1)}, u32[]{:S(2)}, u32[]{:S(2)}) %collective-permute-start.5) | collective-permute-done | bytes 65568 | tf_op jit(solution)/shard_map/ppermute | solution.py:326
  21.3 0.0 copy-done
  21.3 0.0 copy-done.1
  21.3 3.5 %attend.1 = bf16[128,512]{1,0:T(8,128)(2,1)} custom-call(s32[8]{0:T(128)S(1)} %copy-done, s32[1,2]{1,0:T(1,128)S(1)} %copy-done.1, bf16[128,512]{1,0:T(8,128)(2,1)S(1)} %queries.1.q, s32[1,128]{1,0:T(1,128)S(1)} %get-tuple-element.17.caption, bf16[128,256]{1,0:T(8,128)(2,1)S(1)} %get-tuple-element.18.refs_0_, ...), custom_call_target="tpu_custom_call" | custom-call | tf_op jit(solution)/shard_map/attend/pallas_call | solution.py:402
  (2 shorter events, 0.0 us)
Async XLA Ops:
  0.0 6.7 %collective-permute-start.1 = (bf16[128,512]{1,0:T(8,128)(2,1)}, bf16[128,512]{1,0:T(8,128)(2,1)S(1)}, u32[]{:S(2)}, u32[]{:S(2)}) collective-permute-start(bf16[128,512]{1,0:T(8,128)(2,1)} %tokens.1), channel_id=1, source_target_pairs={{0,2},{1,3},{2,0},{3,1},{4,6},{5,7},{6,4},{7,5},{8,10},{9,11},{10,... | collective-permute-start | bytes 393224 | tf_op jit(solution)/shard_map/ppermute | solution.py:326
  3.0 4.0 %collective-permute-start = (bf16[128,512]{1,0:T(8,128)(2,1)}, bf16[128,512]{1,0:T(8,128)(2,1)S(1)}, u32[]{:S(2)}, u32[]{:S(2)}) collective-permute-start(bf16[128,512]{1,0:T(8,128)(2,1)} %tokens.1), channel_id=1, source_target_pairs={{0,1},{1,0},{2,3},{3,2},{4,5},{5,4},{6,7},{7,6},{8,9},{9,8},{10,11... | collective-permute-start | bytes 393224 | tf_op jit(solution)/shard_map/ppermute | solution.py:326
  6.7 1.3 %collective-permute-start.2 = (bf16[128,512]{1,0:T(8,128)(2,1)S(1)}, bf16[128,512]{1,0:T(8,128)(2,1)S(1)}, u32[]{:S(2)}, u32[]{:S(2)}) collective-permute-start(bf16[128,512]{1,0:T(8,128)(2,1)S(1)} %collective-permute-done.1.x2), channel_id=1, source_target_pairs={{0,1},{1,0},{2,3},{3,2},{4,5},{5,4},{6,7},{7,6},{8,9},{9,8},{10,11... | collective-permute-start | bytes 393224 | tf_op jit(solution)/shard_map/ppermute | solution.py:326
  8.0 13.3 %copy-start = (s32[8]{0:T(128)S(1)}, s32[8]{0:T(128)}, u32[]{:S(2)}) copy-start(s32[8]{0:T(128)} %lengths.1) | copy-start | bytes 100
  8.1 13.3 %copy-start.1 = (s32[1,2]{1,0:T(1,128)S(1)}, s32[1,2]{1,0:T(1,128)}, u32[]{:S(2)}) copy-start(s32[1,2]{1,0:T(1,128)} %spans.1) | copy-start | bytes 28
  8.6 5.9 %collective-permute-start.8 = (bf16[128,256]{1,0:T(8,128)(2,1)S(1)}, bf16[128,256]{1,0:T(8,128)(2,1)S(1)}, u32[]{:S(2)}, u32[]{:S(2)}) collective-permute-start(bf16[128,256]{1,0:T(8,128)(2,1)S(1)} %get-tuple-element.18.refs_0_), channel_id=1, source_target_pairs={{0,8},{1,5},{2,10},{3,7},{4,12},{5,1},{6,14},{7,3},{8,0},{9,13},{1... | collective-permute-start | bytes 196616 | tf_op jit(solution)/shard_map/ppermute | solution.py:326
  10.5 7.9 %collective-permute-start.6 = (bf16[128,256]{1,0:T(8,128)(2,1)S(1)}, bf16[128,256]{1,0:T(8,128)(2,1)S(1)}, u32[]{:S(2)}, u32[]{:S(2)}) collective-permute-start(bf16[128,256]{1,0:T(8,128)(2,1)S(1)} %get-tuple-element.18.refs_0_), channel_id=1, source_target_pairs={{0,20},{1,29},{2,22},{3,31},{4,16},{5,25},{6,18},{7,27},{8,28},{9,... | collective-permute-start | bytes 196616 | tf_op jit(solution)/shard_map/ppermute | solution.py:326
  14.0 6.1 %collective-permute-start.4 = (bf16[128,256]{1,0:T(8,128)(2,1)S(1)}, bf16[128,256]{1,0:T(8,128)(2,1)S(1)}, u32[]{:S(2)}, u32[]{:S(2)}) collective-permute-start(bf16[128,256]{1,0:T(8,128)(2,1)S(1)} %get-tuple-element.18.refs_0_), channel_id=1, source_target_pairs={{0,16},{1,25},{2,18},{3,27},{4,20},{5,29},{6,22},{7,31},{8,24},{9,... | collective-permute-start | bytes 196616 | tf_op jit(solution)/shard_map/ppermute | solution.py:326
  14.4 6.6 %collective-permute-start.3 = (bf16[128,256]{1,0:T(8,128)(2,1)S(1)}, bf16[128,256]{1,0:T(8,128)(2,1)S(1)}, u32[]{:S(2)}, u32[]{:S(2)}) collective-permute-start(bf16[128,256]{1,0:T(8,128)(2,1)S(1)} %get-tuple-element.18.refs_0_), channel_id=1, source_target_pairs={{0,12},{1,13},{2,14},{3,15},{4,8},{5,9},{6,10},{7,11},{8,4},{9,5},... | collective-permute-start | bytes 196616 | tf_op jit(solution)/shard_map/ppermute | solution.py:326
  14.6 6.4 %collective-permute-start.9 = (bf16[128,256]{1,0:T(8,128)(2,1)S(1)}, bf16[128,256]{1,0:T(8,128)(2,1)S(1)}, u32[]{:S(2)}, u32[]{:S(2)}) collective-permute-start(bf16[128,256]{1,0:T(8,128)(2,1)S(1)} %collective-permute-done.8.refs_6_), channel_id=1, source_target_pairs={{0,1},{1,0},{2,3},{3,2},{4,5},{5,4},{6,7},{7,6},{8,9},{9,8},{10,11... | collective-permute-start | bytes 196616 | tf_op jit(solution)/shard_map/ppermute | solution.py:326
  18.4 2.5 %collective-permute-start.7 = (bf16[128,256]{1,0:T(8,128)(2,1)S(1)}, bf16[128,256]{1,0:T(8,128)(2,1)S(1)}, u32[]{:S(2)}, u32[]{:S(2)}) collective-permute-start(bf16[128,256]{1,0:T(8,128)(2,1)S(1)} %collective-permute-done.6.refs_4_), channel_id=1, source_target_pairs={{0,1},{1,0},{2,3},{3,2},{4,5},{5,4},{6,7},{7,6},{8,9},{9,8},{10,11... | collective-permute-start | bytes 196616 | tf_op jit(solution)/shard_map/ppermute | solution.py:326
  20.1 1.3 %collective-permute-start.5 = (bf16[128,256]{1,0:T(8,128)(2,1)S(1)}, bf16[128,256]{1,0:T(8,128)(2,1)S(1)}, u32[]{:S(2)}, u32[]{:S(2)}) collective-permute-start(bf16[128,256]{1,0:T(8,128)(2,1)S(1)} %collective-permute-done.4.refs_2_), channel_id=1, source_target_pairs={{0,1},{1,0},{2,3},{3,2},{4,5},{5,4},{6,7},{7,6},{8,9},{9,8},{10,11... | collective-permute-start | bytes 196616 | tf_op jit(solution)/shard_map/ppermute | solution.py:326

commit v3 on v2

--- a/solution.py
+++ b/solution.py
@@ -171,7 +171,7 @@
     )
     allowed = jnp.concatenate([inside(window_first, row_pos, near_pos), span_ok], 1)
     softmax_state = absorb_sliced(start_state, queries, gathered, allowed)
-    highest, denominator, weighted = softmax_state
+    _, denominator, weighted = softmax_state
     return (
         (weighted / denominator[..., None]).reshape(local_rows, head_dev * HD).astype(jnp.bfloat16)
     )
@@ -243,19 +243,67 @@
     kv_out[:, HD:] = both[:, HD:].astype(jnp.bfloat16)
 
 
-def query_kernel(normed, weight, cosine, sine, out):
-    q = jnp.dot(normed[...], weight[...], preferred_element_type=jnp.float32)
+def block_of(offset):
+    odd = lax.rem(lax.axis_index("head"), 2)
+    return jnp.bitwise_xor(lax.axis_index("seq"), offset[0] + odd * (offset[1] - offset[0]))
+
+
+def fold(q, bias, columns, kv, scores, rounded, old, new):
+    rows = bias.shape[0]
+    for i, block in enumerate(kv):
+        scores[:, i * BLOCK : (i + 1) * BLOCK] = lax.dot_general(
+            q[...],
+            block[:, :HD],
+            (((1,), (1,)), ((), ())),
+            preferred_element_type=jnp.float32,
+        )
+    width = len(kv) * BLOCK
+    for begin in range(0, q.shape[0], rows):
+        part = slice(begin, begin + rows)
+        s = scores[part, :width] + jnp.concatenate([bias[:, c : c + BLOCK] for c in columns], 1)
+        highest = jnp.broadcast_to(jnp.max(s, -1, keepdims=True), (rows, BLOCK))
+        if old is not None:
+            highest = jnp.maximum(highest, old[0][part, :])
+        total = None
+        for i in range(len(kv)):
+            piece = slice(i * BLOCK, (i + 1) * BLOCK)
+            weights = jnp.exp(s[:, piece] - highest)
+            rounded[part, piece] = weights.astype(jnp.bfloat16)
+            total = weights if total is None else total + weights
+        mixed = None
+        for i, block in enumerate(kv):
+            piece = slice(i * BLOCK, (i + 1) * BLOCK)
+            product = jnp.dot(
+                rounded[part, piece], block[:, HD:], preferred_element_type=jnp.float32
+            )
+            mixed = product if mixed is None else mixed + product
+        if old is not None:
+            rescale = jnp.exp(old[0][part, :] - highest)
+            total = total + rescale * old[1][part, :]
+            mixed = mixed + rescale * old[2][part, :]
+        new(begin // rows, part, highest, total, mixed)
+
+
+def keep(state):
+    def new(_, part, *values):
+        for ref, value in zip(state, values):
+            ref[part, :] = value
+
+    return new
+
+
+def query_kernel(
+    offsets, lengths, spans, normed, weight, cosine, sine, caption, own, *refs
+):
+    (q, bias), state, (scores, rounded) = refs[:2], refs[2:5], refs[5:]
+    rows = normed.shape[0]
+    rank = lax.axis_index("seq")
+    product = jnp.dot(normed[...], weight[...], preferred_element_type=jnp.float32)
     c, s = tables(cosine, sine)
-    for begin in range(0, q.shape[1], HD):
-        turned = turn(q[:, begin : begin + HD], c, s)
-        out[:, begin : begin + HD] = (turned * HD ** (-0.5)).astype(jnp.bfloat16)
-
-
-def attend_kernel(offsets, lengths, spans, q, caption, *refs):
-    blocks = len(offsets)
-    kv, (out, scores, bias) = refs[:blocks], refs[blocks:]
-    rows = q.shape[0]
-    rank, odd = lax.axis_index("seq"), lax.rem(lax.axis_index("head"), 2)
+    for begin in range(0, product.shape[1], HD):
+        turned = turn(product[:, begin : begin + HD], c, s)
+        first = begin // HD * rows
+        q[first : first + rows, :] = (turned * HD ** (-0.5)).astype(jnp.bfloat16)
     row_pos = rank * rows + lax.broadcasted_iota(jnp.int32, (rows, BLOCK), 0)
     first_row = jnp.zeros((rows, BLOCK), jnp.int32)
     begin = jnp.int32(0)
@@ -265,41 +313,31 @@
         first_row = jnp.where(within, begin, first_row)
         begin = end
     is_caption = jnp.broadcast_to(caption[...], (rows, rows)).T == 1
-    for order, (even_offset, odd_offset) in enumerate(offsets):
-        offset = even_offset + odd * (odd_offset - even_offset)
-        block = jnp.bitwise_xor(rank, offset)
+    for order, offset in enumerate(offsets):
+        block = block_of(offset)
         key_pos = block * BLOCK + lax.broadcasted_iota(jnp.int32, (rows, BLOCK), 1)
         near = (first_row <= key_pos) & (key_pos <= row_pos)
         reached = (spans[0, 0] <= block) & (block <= spans[0, 1])
         allowed = near | (is_caption & reached)
         bias[:, order * BLOCK : (order + 1) * BLOCK] = jnp.where(allowed, 0.0, -jnp.inf)
-    for head in range(q.shape[1] // HD):
-        qh = q[:, head * HD : (head + 1) * HD]
-        for order in range(blocks):
-            columns = slice(order * BLOCK, (order + 1) * BLOCK)
-            scores[:, columns] = (
-                lax.dot_general(
-                    qh,
-                    kv[order][:, :HD],
-                    (((1,), (1,)), ((), ())),
-                    preferred_element_type=jnp.float32,
-                )
-                + bias[:, columns]
-            )
-        s = scores[...]
-        highest = jnp.max(s, -1, keepdims=True)
-        weights = jnp.exp(s - highest)
-        denominator = jnp.sum(weights, -1, keepdims=True)
-        rounded = weights.astype(jnp.bfloat16)
-        mixed = None
-        for order in range(blocks):
-            part = jnp.dot(
-                rounded[:, order * BLOCK : (order + 1) * BLOCK],
-                kv[order][:, HD:],
-                preferred_element_type=jnp.float32,
-            )
-            mixed = part if mixed is None else mixed + part
+    fold(q, bias, [0], [own], scores, rounded, None, keep(state))
+
+
+def middle_kernel(columns, q, bias, *refs):
+    old, kv = refs[:3], refs[3 : 3 + len(columns)]
+    state, (scores, rounded) = refs[3 + len(columns) : 6 + len(columns)], refs[6 + len(columns) :]
+    fold(q, bias, columns, kv, scores, rounded, old, keep(state))
+
+
+def last_kernel(columns, q, bias, *refs):
+    old, kv = refs[:3], refs[3 : 3 + len(columns)]
+    out, scores, rounded = refs[3 + len(columns) :]
+
+    def new(head, _, highest, total, mixed):
+        denominator = jnp.sum(total, -1, keepdims=True)
         out[:, head * HD : (head + 1) * HD] = (mixed / denominator).astype(jnp.bfloat16)
+
+    fold(q, bias, columns, kv, scores, rounded, old, new)
 
 
 def everywhere(
@@ -384,39 +422,82 @@
     )
 
     far = ranks // 2
-    plan = [(far, far | 2), (far | 1, far | 3), (2, 1)]
-    fetched = [move(key_values, lambda g, both=both: (both[g % 2], 0)) for both in plan]
-    last = move(key_values, lambda g: (3, 0))
-    queries = pl.pallas_call(
-        query_kernel,
-        out_shape=pltpu.VMEM((rows, head_dev * HD), jnp.bfloat16),
-        in_specs=vmem(4),
-        out_specs=vmem(1)[0],
-        compiler_params=grant(4),
+    tall = rows * head_dev
+
+    def swapped(array):
+        return move(array, lambda g: (0, 1))
+
+    def split(array, both):
+        return move(array, lambda g: (both[g % 2], 0))
+
+    column = split(key_values, (far, far | 2))
+    row = split(key_values, (2, 1))
+    corner = split(key_values, (3, 3))
+    diagonal = split(key_values, (far | 1, far | 3))
+    held = [
+        ((0, 0), key_values),
+        ((2, 1), row),
+        ((1, 2), swapped(row)),
+        ((far, far | 2), column),
+        ((far | 2, far), swapped(column)),
+        ((3, 3), corner),
+        ((far | 1, far | 3), diagonal),
+        ((far | 3, far | 1), swapped(diagonal)),
+    ]
+    offsets, arrays = [offset for offset, _ in held], [near_core(array) for _, array in held]
+    state = [pltpu.VMEM((tall, BLOCK), jnp.float32)] * 2 + [pltpu.VMEM((tall, HD), jnp.float32)]
+
+    def work(count):
+        return [
+            pltpu.VMEM((tall, count * BLOCK), jnp.float32),
+            pltpu.VMEM((tall, count * BLOCK), jnp.bfloat16),
+        ]
+
+    q, bias, *partial = pl.pallas_call(
+        functools.partial(query_kernel, offsets),
+        out_shape=(
+            pltpu.VMEM((tall, HD), jnp.bfloat16),
+            pltpu.VMEM((rows, ranks * BLOCK), jnp.float32),
+            *state,
+        ),
+        in_specs=smem(2) + vmem(6),
+        out_specs=tuple(vmem(5)),
+        scratch_shapes=work(1),
+        compiler_params=grant(6),
         name="queries",
-    )(near_core(normed), near_core(wide), cosine, sine)
-    offsets, held = [(0, 0), (3, 3)], [key_values, last]
-    for both, own in zip(plan, fetched):
-        offsets += [both, both[::-1]]
-        held += [own, move(own, lambda g: (0, 1))]
-    return pl.pallas_call(
-        functools.partial(attend_kernel, offsets),
-        out_shape=jax.ShapeDtypeStruct((rows, head_dev * HD), jnp.bfloat16),
-        in_specs=smem(2) + vmem(2 + ranks),
-        out_specs=vmem(1)[0],
-        scratch_shapes=[
-            pltpu.VMEM((rows, ranks * BLOCK), jnp.float32),
-            pltpu.VMEM((rows, ranks * BLOCK), jnp.float32),
-        ],
-        compiler_params=grant(8),
-        name="attend",
     )(
         window_lengths,
         span_blocks,
-        near_core(queries),
+        near_core(normed),
+        near_core(wide),
+        cosine,
+        sine,
         near_core(captions),
-        *[near_core(array) for array in held],
-    )
+        arrays[0],
+    )
+
+    def columns(first, end):
+        return [order * BLOCK for order in range(first, end)]
+
+    later = ranks - 3
+    partial = pl.pallas_call(
+        functools.partial(middle_kernel, columns(1, later)),
+        out_shape=tuple(state),
+        in_specs=vmem(5 + later - 1),
+        out_specs=tuple(vmem(3)),
+        scratch_shapes=work(later - 1),
+        compiler_params=grant(6),
+        name="middle",
+    )(*[near_core(array) for array in (q, bias, *partial)], *arrays[1:later])
+    return pl.pallas_call(
+        functools.partial(last_kernel, columns(later, ranks)),
+        out_shape=jax.ShapeDtypeStruct((rows, head_dev * HD), jnp.bfloat16),
+        in_specs=vmem(5 + ranks - later),
+        out_specs=vmem(1)[0],
+        scratch_shapes=work(ranks - later),
+        compiler_params=grant(6),
+        name="last",
+    )(*[near_core(array) for array in (q, bias, *partial)], *arrays[later:])
 
 
 def solution(mesh):

time: 24.9 us -> 24.4 us (0.980)
  waiting for transfers between devices: 8.81 us -> 5.5 us
  starting transfers between devices: 8.92 us -> 11.9 us
  Pallas kernels: 6.69 us -> 6.34 us
    ppermute x10, waiting for transfers between devices: 8.81 us -> 5.5 us  [move(): return lax.ppermute(array, ('seq', 'head'), pairs)]
    ppermute x10, starting transfers between devices: 8.92 us -> 11.9 us  [move(): return lax.ppermute(array, ('seq', 'head'), pairs)]
    pallas_call x2 -> x3, Pallas kernels: 4.04 us -> 3.7 us  [the longest x1 1.63 us: everywhere(): pl.pallas_call(functools.partial(query_kernel, offsets), out_shape=(pltpu...]
  transfers between devices with their start and end apart: 10 -> 10, of which waited for: 6 -> 5; matrix products, arithmetic and copies ran while one was open for 1% -> 1% of each run, Pallas kernels for 11% -> 18%
where the time goes in v3:
time: 24.4 us; the launch traced here: 24.2 us
  starting transfers between devices  11.9 us (49%)
  Pallas kernels  6.34 us (26%)
  waiting for transfers between devices  5.5 us (23%)
  other arithmetic  0.32 us (1%)
    ppermute x10, starting transfers between devices, move(): return lax.ppermute(array, ('seq', 'head'), pairs)  11.9 us
    ppermute x10, waiting for transfers between devices, move(): return lax.ppermute(array, ('seq', 'head'), pairs)  5.5 us
    pallas_call x1, Pallas kernels, everywhere(): pl.pallas_call(functools.partial(load_kernel, H // KV // head_dev), out_s...  2.07 us
    pallas_call x1, Pallas kernels, everywhere(): pl.pallas_call(functools.partial(query_kernel, offsets), out_shape=(pltpu...  1.63 us
    pallas_call x1, Pallas kernels, everywhere(): pl.pallas_call(functools.partial(last_kernel, columns(later, ranks)), out...  1.34 us
    pallas_call x1, Pallas kernels, everywhere(): pl.pallas_call(functools.partial(middle_kernel, columns(1, later)), out_s...  0.73 us
    pallas_call x1, Pallas kernels, everywhere(): pl.pallas_call(kv_kernel, out_shape=(pltpu.VMEM((rows, 2 * HD), jnp.bfloa...  0.58 us
  transfers between devices with their start and end apart: 10, of which 5 were waited for; matrix products, arithmetic and copies ran while one was open for 1% of the time, Pallas kernels for 18%

profile of v3, /device:TPU:0, one launch (start us, length us, event | category | flops | bytes accessed | tf_op | source)
XLA Modules:
  0.0 24.2 jit_solution(14263018959495815063)
XLA Ops:
  0.0 3.0 %collective-permute-start.1 = (bf16[128,512]{1,0:T(8,128)(2,1)}, bf16[128,512]{1,0:T(8,128)(2,1)S(1)}, u32[]{:S(2)}, u32[]{:S(2)}) collective-permute-start(bf16[128,512]{1,0:T(8,128)(2,1)} %tokens.1), channel_id=1, source_target_pairs={{0,2},{1,3},{2,0},{3,1},{4,6},{5,7},{6,4},{7,5},{8,10},{9,11},{10,... | collective-permute-start | bytes 393224 | tf_op jit(solution)/shard_map/ppermute | solution.py:364
  3.0 0.0 collective-permute-start
  3.0 0.0 copy-start
  3.0 0.0 copy-start.1
  3.0 2.1 %load.1 = (bf16[128,512]{1,0:T(8,128)(2,1)S(1)}, f32[1,2048]{1,0:T(1,128)S(1)}, bf16[2048,256]{1,0:T(8,128)(2,1)S(1)}, bf16[2048,512]{1,0:T(8,128)(2,1)S(1)}, s32[1,128]{1,0:T(1,128)S(1)}) custom-call(bf16[128,512]{1,0:T(8,128)(2,1)} %tokens.1, f32[1,2048]{1,0:T(1,128)} %bitcast.2, bf16[2048,256]{1,0:T(8,128)(2,1)} %key_weight.1, ...), custom_call_target="tpu_custom_call" | custom-call | tf_op jit(solution)/shard_map/load/pallas_call | solution.py:369
  5.1 1.6 %collective-permute-done.1.x2 = bf16[128,512]{1,0:T(8,128)(2,1)S(1)} collective-permute-done((bf16[128,512]{1,0:T(8,128)(2,1)}, bf16[128,512]{1,0:T(8,128)(2,1)S(1)}, u32[]{:S(2)}, u32[]{:S(2)}) %collective-permute-start.1) | collective-permute-done | bytes 131104 | tf_op jit(solution)/shard_map/ppermute | solution.py:364
  6.7 0.0 collective-permute-start.2
  6.7 0.3 %multiply_sine_fusion = (f32[128,64]{1,0:T(8,128)S(1)}, f32[128,64]{1,0:T(8,128)S(1)}) fusion(f32[64]{0:T(128)S(1)} %multiply_power_fusion, f32[128]{0:T(128)S(1)} %add_convert_fusion), kind=kLoop, calls=%fused_computation | loop fusion | flops 8192 | bytes 66304 | tf_op jit(solution)/shard_map/sin | solution.py:400
  7.0 0.0 collective-permute-done.x1
  7.0 1.0 %collective-permute-done.2.x3 = bf16[128,512]{1,0:T(8,128)(2,1)S(1)} collective-permute-done((bf16[128,512]{1,0:T(8,128)(2,1)S(1)}, bf16[128,512]{1,0:T(8,128)(2,1)S(1)}, u32[]{:S(2)}, u32[]{:S(2)}) %collective-permute-start.2) | collective-permute-done | bytes 131104 | tf_op jit(solution)/shard_map/ppermute | solution.py:364
  8.0 0.6 %keys_values.1 = (bf16[128,256]{1,0:T(8,128)(2,1)S(1)}, bf16[128,2048]{1,0:T(8,128)(2,1)S(1)}) custom-call(bf16[128,512]{1,0:T(8,128)(2,1)S(1)} %get-tuple-element.20.x0, bf16[128,512]{1,0:T(8,128)(2,1)S(1)} %collective-permute-done.x1, bf16[128,512]{1,0:T(8,128)(2,1)S(1)} %collective-permute-done.1.x2, bf16[128,512]{1,0:T(8,128)(2,1)S(1)} %collective-permute-done.2.x3, ...), custom_call_target="tpu_custom_call" | custom-call | tf_op jit(solution)/shard_map/keys_values/pallas_call | solution.py:403
  8.6 2.9 %collective-permute-start.5 = (bf16[128,256]{1,0:T(8,128)(2,1)S(1)}, bf16[128,256]{1,0:T(8,128)(2,1)S(1)}, u32[]{:S(2)}, u32[]{:S(2)}) collective-permute-start(bf16[128,256]{1,0:T(8,128)(2,1)S(1)} %get-tuple-element.26.own), channel_id=1, source_target_pairs={{0,16},{1,25},{2,18},{3,27},{4,20},{5,29},{6,22},{7,31},{8,24},{9,... | collective-permute-start | bytes 196616 | tf_op jit(solution)/shard_map/ppermute | solution.py:364
  11.5 1.6 %collective-permute-start.3 = (bf16[128,256]{1,0:T(8,128)(2,1)S(1)}, bf16[128,256]{1,0:T(8,128)(2,1)S(1)}, u32[]{:S(2)}, u32[]{:S(2)}) collective-permute-start(bf16[128,256]{1,0:T(8,128)(2,1)S(1)} %get-tuple-element.26.own), channel_id=1, source_target_pairs={{0,8},{1,5},{2,10},{3,7},{4,12},{5,1},{6,14},{7,3},{8,0},{9,13},{1... | collective-permute-start | bytes 196616 | tf_op jit(solution)/shard_map/ppermute | solution.py:364
  13.1 1.3 %collective-permute-start.8 = (bf16[128,256]{1,0:T(8,128)(2,1)S(1)}, bf16[128,256]{1,0:T(8,128)(2,1)S(1)}, u32[]{:S(2)}, u32[]{:S(2)}) collective-permute-start(bf16[128,256]{1,0:T(8,128)(2,1)S(1)} %get-tuple-element.26.own), channel_id=1, source_target_pairs={{0,20},{1,29},{2,22},{3,31},{4,16},{5,25},{6,18},{7,27},{8,28},{9,... | collective-permute-start | bytes 196616 | tf_op jit(solution)/shard_map/ppermute | solution.py:364
  14.4 1.5 %collective-permute-done.5.refs_5_ = bf16[128,256]{1,0:T(8,128)(2,1)S(1)} collective-permute-done((bf16[128,256]{1,0:T(8,128)(2,1)S(1)}, bf16[128,256]{1,0:T(8,128)(2,1)S(1)}, u32[]{:S(2)}, u32[]{:S(2)}) %collective-permute-start.5) | collective-permute-done | bytes 65568 | tf_op jit(solution)/shard_map/ppermute | solution.py:364
  15.8 0.0 collective-permute-start.6
  15.8 0.3 %collective-permute-done.3.refs_3_ = bf16[128,256]{1,0:T(8,128)(2,1)S(1)} collective-permute-done((bf16[128,256]{1,0:T(8,128)(2,1)S(1)}, bf16[128,256]{1,0:T(8,128)(2,1)S(1)}, u32[]{:S(2)}, u32[]{:S(2)}) %collective-permute-start.3) | collective-permute-done | bytes 65568 | tf_op jit(solution)/shard_map/ppermute | solution.py:364
  16.2 0.2 collective-permute-start.4
  16.3 3.0 %collective-permute-start.7 = (bf16[128,256]{1,0:T(8,128)(2,1)S(1)}, bf16[128,256]{1,0:T(8,128)(2,1)S(1)}, u32[]{:S(2)}, u32[]{:S(2)}) collective-permute-start(bf16[128,256]{1,0:T(8,128)(2,1)S(1)} %get-tuple-element.26.own), channel_id=1, source_target_pairs={{0,12},{1,13},{2,14},{3,15},{4,8},{5,9},{6,10},{7,11},{8,4},{9,5},... | collective-permute-start | bytes 196616 | tf_op jit(solution)/shard_map/ppermute | solution.py:364
  19.4 1.1 %collective-permute-done.8.refs_4_ = bf16[128,256]{1,0:T(8,128)(2,1)S(1)} collective-permute-done((bf16[128,256]{1,0:T(8,128)(2,1)S(1)}, bf16[128,256]{1,0:T(8,128)(2,1)S(1)}, u32[]{:S(2)}, u32[]{:S(2)}) %collective-permute-start.8) | collective-permute-done | bytes 65568 | tf_op jit(solution)/shard_map/ppermute | solution.py:364
  20.5 0.0 collective-permute-start.9
  20.5 0.0 copy-done
  20.5 0.0 copy-done.1
  20.5 1.6 %queries.1 = (bf16[512,128]{1,0:T(8,128)(2,1)S(1)}, f32[128,1024]{1,0:T(8,128)S(1)}, f32[512,128]{1,0:T(8,128)S(1)}, f32[512,128]{1,0:T(8,128)S(1)}, f32[512,128]{1,0:T(8,128)S(1)}) custom-call(s32[8]{0:T(128)S(1)} %copy-done, s32[1,2]{1,0:T(1,128)S(1)} %copy-done.1, bf16[128,2048]{1,0:T(8,128)(2,1)S(1)} %get-tuple-element.23.normed, ...), custom_call_target="tpu_custom_call" | custom-call | tf_op jit(solution)/shard_map/queries/pallas_call | solution.py:456
  22.1 0.0 collective-permute-done.6.refs_6_
  22.1 0.0 collective-permute-done.4.refs_4_
  22.1 0.7 %middle.1 = (f32[512,128]{1,0:T(8,128)S(1)}, f32[512,128]{1,0:T(8,128)S(1)}, f32[512,128]{1,0:T(8,128)S(1)}) custom-call(bf16[512,128]{1,0:T(8,128)(2,1)S(1)} %get-tuple-element.27.q, f32[128,1024]{1,0:T(8,128)S(1)} %get-tuple-element.28.bias, f32[512,128]{1,0:T(8,128)S(1)} %get-tuple-element.29.refs_0_, f32[512,128]{1,0:T(8,128)S(1)} %get-tuple-element.30.refs_1_, ...), custom_call_target="tpu_custom_call" | custom-call | tf_op jit(solution)/shard_map/middle/pallas_call | solution.py:483
  22.9 0.0 collective-permute-done.7.refs_3_
  22.9 0.0 collective-permute-done.9.refs_5_
  22.9 1.3 %last.1 = bf16[128,512]{1,0:T(8,128)(2,1)} custom-call(bf16[512,128]{1,0:T(8,128)(2,1)S(1)} %get-tuple-element.27.q, f32[128,1024]{1,0:T(8,128)S(1)} %get-tuple-element.28.bias, f32[512,128]{1,0:T(8,128)S(1)} %get-tuple-element.32.refs_0_, f32[512,128]{1,0:T(8,128)S(1)} %get-tuple-element.33.refs_1_, f32[512,128]{1,0:T(8,128)S(1)} %get-tuple-element.34.refs_2_, ...), custom_call_target="tpu_custom_call" | custom-call | tf_op jit(solution)/shard_map/last/pallas_call | solution.py:492
  (2 shorter events, 0.0 us)
Async XLA Ops:
  0.0 6.7 %collective-permute-start.1 = (bf16[128,512]{1,0:T(8,128)(2,1)}, bf16[128,512]{1,0:T(8,128)(2,1)S(1)}, u32[]{:S(2)}, u32[]{:S(2)}) collective-permute-start(bf16[128,512]{1,0:T(8,128)(2,1)} %tokens.1), channel_id=1, source_target_pairs={{0,2},{1,3},{2,0},{3,1},{4,6},{5,7},{6,4},{7,5},{8,10},{9,11},{10,... | collective-permute-start | bytes 393224 | tf_op jit(solution)/shard_map/ppermute | solution.py:364
  3.0 4.0 %collective-permute-start = (bf16[128,512]{1,0:T(8,128)(2,1)}, bf16[128,512]{1,0:T(8,128)(2,1)S(1)}, u32[]{:S(2)}, u32[]{:S(2)}) collective-permute-start(bf16[128,512]{1,0:T(8,128)(2,1)} %tokens.1), channel_id=1, source_target_pairs={{0,1},{1,0},{2,3},{3,2},{4,5},{5,4},{6,7},{7,6},{8,9},{9,8},{10,11... | collective-permute-start | bytes 393224 | tf_op jit(solution)/shard_map/ppermute | solution.py:364
  3.0 17.5 %copy-start = (s32[8]{0:T(128)S(1)}, s32[8]{0:T(128)}, u32[]{:S(2)}) copy-start(s32[8]{0:T(128)} %lengths.1) | copy-start | bytes 100
  3.0 17.4 %copy-start.1 = (s32[1,2]{1,0:T(1,128)S(1)}, s32[1,2]{1,0:T(1,128)}, u32[]{:S(2)}) copy-start(s32[1,2]{1,0:T(1,128)} %spans.1) | copy-start | bytes 28
  6.7 1.3 %collective-permute-start.2 = (bf16[128,512]{1,0:T(8,128)(2,1)S(1)}, bf16[128,512]{1,0:T(8,128)(2,1)S(1)}, u32[]{:S(2)}, u32[]{:S(2)}) collective-permute-start(bf16[128,512]{1,0:T(8,128)(2,1)S(1)} %collective-permute-done.1.x2), channel_id=1, source_target_pairs={{0,1},{1,0},{2,3},{3,2},{4,5},{5,4},{6,7},{7,6},{8,9},{9,8},{10,11... | collective-permute-start | bytes 393224 | tf_op jit(solution)/shard_map/ppermute | solution.py:364
  8.6 7.2 %collective-permute-start.5 = (bf16[128,256]{1,0:T(8,128)(2,1)S(1)}, bf16[128,256]{1,0:T(8,128)(2,1)S(1)}, u32[]{:S(2)}, u32[]{:S(2)}) collective-permute-start(bf16[128,256]{1,0:T(8,128)(2,1)S(1)} %get-tuple-element.26.own), channel_id=1, source_target_pairs={{0,16},{1,25},{2,18},{3,27},{4,20},{5,29},{6,22},{7,31},{8,24},{9,... | collective-permute-start | bytes 196616 | tf_op jit(solution)/shard_map/ppermute | solution.py:364
  11.5 4.6 %collective-permute-start.3 = (bf16[128,256]{1,0:T(8,128)(2,1)S(1)}, bf16[128,256]{1,0:T(8,128)(2,1)S(1)}, u32[]{:S(2)}, u32[]{:S(2)}) collective-permute-start(bf16[128,256]{1,0:T(8,128)(2,1)S(1)} %get-tuple-element.26.own), channel_id=1, source_target_pairs={{0,8},{1,5},{2,10},{3,7},{4,12},{5,1},{6,14},{7,3},{8,0},{9,13},{1... | collective-permute-start | bytes 196616 | tf_op jit(solution)/shard_map/ppermute | solution.py:364
  13.1 7.4 %collective-permute-start.8 = (bf16[128,256]{1,0:T(8,128)(2,1)S(1)}, bf16[128,256]{1,0:T(8,128)(2,1)S(1)}, u32[]{:S(2)}, u32[]{:S(2)}) collective-permute-start(bf16[128,256]{1,0:T(8,128)(2,1)S(1)} %get-tuple-element.26.own), channel_id=1, source_target_pairs={{0,20},{1,29},{2,22},{3,31},{4,16},{5,25},{6,18},{7,27},{8,28},{9,... | collective-permute-start | bytes 196616 | tf_op jit(solution)/shard_map/ppermute | solution.py:364
  15.8 6.3 %collective-permute-start.6 = (bf16[128,256]{1,0:T(8,128)(2,1)S(1)}, bf16[128,256]{1,0:T(8,128)(2,1)S(1)}, u32[]{:S(2)}, u32[]{:S(2)}) collective-permute-start(bf16[128,256]{1,0:T(8,128)(2,1)S(1)} %collective-permute-done.5.refs_5_), channel_id=1, source_target_pairs={{0,1},{1,0},{2,3},{3,2},{4,5},{5,4},{6,7},{7,6},{8,9},{9,8},{10,11... | collective-permute-start | bytes 196616 | tf_op jit(solution)/shard_map/ppermute | solution.py:364
  16.2 6.0 %collective-permute-start.4 = (bf16[128,256]{1,0:T(8,128)(2,1)S(1)}, bf16[128,256]{1,0:T(8,128)(2,1)S(1)}, u32[]{:S(2)}, u32[]{:S(2)}) collective-permute-start(bf16[128,256]{1,0:T(8,128)(2,1)S(1)} %collective-permute-done.3.refs_3_), channel_id=1, source_target_pairs={{0,1},{1,0},{2,3},{3,2},{4,5},{5,4},{6,7},{7,6},{8,9},{9,8},{10,11... | collective-permute-start | bytes 196616 | tf_op jit(solution)/shard_map/ppermute | solution.py:364
  16.3 6.5 %collective-permute-start.7 = (bf16[128,256]{1,0:T(8,128)(2,1)S(1)}, bf16[128,256]{1,0:T(8,128)(2,1)S(1)}, u32[]{:S(2)}, u32[]{:S(2)}) collective-permute-start(bf16[128,256]{1,0:T(8,128)(2,1)S(1)} %get-tuple-element.26.own), channel_id=1, source_target_pairs={{0,12},{1,13},{2,14},{3,15},{4,8},{5,9},{6,10},{7,11},{8,4},{9,5},... | collective-permute-start | bytes 196616 | tf_op jit(solution)/shard_map/ppermute | solution.py:364
  20.5 2.4 %collective-permute-start.9 = (bf16[128,256]{1,0:T(8,128)(2,1)S(1)}, bf16[128,256]{1,0:T(8,128)(2,1)S(1)}, u32[]{:S(2)}, u32[]{:S(2)}) collective-permute-start(bf16[128,256]{1,0:T(8,128)(2,1)S(1)} %collective-permute-done.8.refs_4_), channel_id=1, source_target_pairs={{0,1},{1,0},{2,3},{3,2},{4,5},{5,4},{6,7},{7,6},{8,9},{9,8},{10,11... | collective-permute-start | bytes 196616 | tf_op jit(solution)/shard_map/ppermute | solution.py:364

commit v4 on v3

--- a/solution.py
+++ b/solution.py
@@ -221,15 +221,27 @@
         copy.wait()
 
 
-def kv_kernel(x0, x1, x2, x3, gain, weight, cosine, sine, kv_out, normed_out):
+def squares_kernel(*refs):
+    parts, out = refs[:-1], refs[-1]
+    total = None
+    for part in parts:
+        hidden = part[...].astype(jnp.float32)
+        for begin in range(0, hidden.shape[1], out.shape[1]):
+            piece = hidden[:, begin : begin + out.shape[1]]
+            total = piece * piece if total is None else total + piece * piece
+    out[...] = total
+
+
+def kv_kernel(squares, x0, x1, x2, x3, gain, weight, cosine, sine, kv_out, normed_out):
     depth = x0.shape[1]
     parts = (x0, x1, x2, x3)
     me = lax.axis_index("head")
-    total = None
-    for part in parts:
-        hidden = part[...].astype(jnp.float32)
-        squares = jnp.sum(hidden * hidden, -1, keepdims=True)
-        total = squares if total is None else total + squares
+    hidden = x3[...].astype(jnp.float32)
+    total = squares[...]
+    for begin in range(0, depth, total.shape[1]):
+        piece = hidden[:, begin : begin + total.shape[1]]
+        total = total + piece * piece
+    total = jnp.sum(total, -1, keepdims=True)
     scale = lax.rsqrt(total / (depth * len(parts)) + norm_eps)
     both = None
     for order, part in enumerate(parts):
@@ -250,14 +262,14 @@
 
 def fold(q, bias, columns, kv, scores, rounded, old, new):
     rows = bias.shape[0]
-    for i, block in enumerate(kv):
-        scores[:, i * BLOCK : (i + 1) * BLOCK] = lax.dot_general(
-            q[...],
-            block[:, :HD],
-            (((1,), (1,)), ((), ())),
-            preferred_element_type=jnp.float32,
-        )
+    scores[...] = lax.dot_general(
+        q[...],
+        jnp.concatenate([block[:, :HD] for block in kv], 0),
+        (((1,), (1,)), ((), ())),
+        preferred_element_type=jnp.float32,
+    )
     width = len(kv) * BLOCK
+    highs, totals = [], []
     for begin in range(0, q.shape[0], rows):
         part = slice(begin, begin + rows)
         s = scores[part, :width] + jnp.concatenate([bias[:, c : c + BLOCK] for c in columns], 1)
@@ -270,18 +282,18 @@
             weights = jnp.exp(s[:, piece] - highest)
             rounded[part, piece] = weights.astype(jnp.bfloat16)
             total = weights if total is None else total + weights
-        mixed = None
-        for i, block in enumerate(kv):
-            piece = slice(i * BLOCK, (i + 1) * BLOCK)
-            product = jnp.dot(
-                rounded[part, piece], block[:, HD:], preferred_element_type=jnp.float32
-            )
-            mixed = product if mixed is None else mixed + product
+        highs.append(highest)
+        totals.append(total)
+    stacked = jnp.concatenate([block[:, HD:] for block in kv], 0)
+    mixed = jnp.dot(rounded[:, :width], stacked, preferred_element_type=jnp.float32)
+    for head, (highest, total) in enumerate(zip(highs, totals)):
+        part = slice(head * rows, (head + 1) * rows)
+        out = mixed[part, :]
         if old is not None:
             rescale = jnp.exp(old[0][part, :] - highest)
             total = total + rescale * old[1][part, :]
-            mixed = mixed + rescale * old[2][part, :]
-        new(begin // rows, part, highest, total, mixed)
+            out = out + rescale * old[2][part, :]
+        new(head, part, highest, total, out)
 
 
 def keep(state):
@@ -366,7 +378,7 @@
     across = move(tokens, lambda g: (0, 2))
     beside = move(tokens, lambda g: (0, 1))
     features = query_weight.shape[0]
-    row, gain, kv_weight, wide, captions = pl.pallas_call(
+    token_copy, gain, kv_weight, wide, captions = pl.pallas_call(
         functools.partial(load_kernel, H // KV // head_dev),
         out_shape=(
             pltpu.VMEM(tokens.shape, tokens.dtype),
@@ -398,23 +410,32 @@
     row_pos = rank * rows + jnp.arange(rows, dtype=jnp.int32)
     angles = row_pos.astype(jnp.float32)[:, None] * frequency[None, :]
     cosine, sine = near_core(jnp.cos(angles)), near_core(jnp.sin(angles))
-    corner = move(across, lambda g: (0, 1))
-
+    fourth = move(across, lambda g: (0, 1))
+
+    squares = pl.pallas_call(
+        squares_kernel,
+        out_shape=pltpu.VMEM((rows, HD), jnp.float32),
+        in_specs=vmem(3),
+        out_specs=vmem(1)[0],
+        compiler_params=grant(2),
+        name="squares",
+    )(near_core(token_copy), near_core(beside), near_core(across))
     key_values, normed = pl.pallas_call(
         kv_kernel,
         out_shape=(
             pltpu.VMEM((rows, 2 * HD), jnp.bfloat16),
             pltpu.VMEM((rows, features), jnp.bfloat16),
         ),
-        in_specs=vmem(8),
+        in_specs=vmem(9),
         out_specs=tuple(vmem(2)),
         compiler_params=grant(6),
         name="keys_values",
     )(
-        near_core(row),
+        near_core(squares),
+        near_core(token_copy),
         near_core(beside),
         near_core(across),
-        near_core(corner),
+        near_core(fourth),
         near_core(gain),
         near_core(kv_weight),
         cosine,
@@ -440,8 +461,8 @@
         ((1, 2), swapped(row)),
         ((far, far | 2), column),
         ((far | 2, far), swapped(column)),
+        ((far | 1, far | 3), diagonal),
         ((3, 3), corner),
-        ((far | 1, far | 3), diagonal),
         ((far | 3, far | 1), swapped(diagonal)),
     ]
     offsets, arrays = [offset for offset, _ in held], [near_core(array) for _, array in held]
@@ -479,7 +500,7 @@
     def columns(first, end):
         return [order * BLOCK for order in range(first, end)]
 
-    later = ranks - 3
+    later = ranks - 2
     partial = pl.pallas_call(
         functools.partial(middle_kernel, columns(1, later)),
         out_shape=tuple(state),
@@ -500,17 +521,29 @@
     )(*[near_core(array) for array in (q, bias, *partial)], *arrays[later:])
 
 
+near_plan = (0, 1, 2, 3)
+feature_plan = (0, 1, 2, 3)
+
+
+def gathers_all(mesh, rows, head_dev):
+    ranks, groups = mesh.shape["seq"], mesh.shape["head"]
+    total_blocks = ranks * rows // BLOCK
+    window = min(window_cap, total_blocks * BLOCK // 4)
+    read = (window + BLOCK - 2) // BLOCK + 1 + min(span_cap, total_blocks // 4)
+    shared = groups % 2 == 0 and (H // KV) % (2 * head_dev) == 0
+    fits = rows == BLOCK and ranks == 2 * len(near_plan) and groups == len(feature_plan)
+    return shared and fits and 2 * read >= total_blocks
+
+
 def solution(mesh):
-    ranks, groups = mesh.shape["seq"], mesh.shape["head"]
     in_specs = (P("seq", "head"), P(), P(None, "head"), P(), P(), P(), P("seq"), P("seq", None))
     out_specs = P("seq", "head")
 
     def per_device(*arguments):
-        rows = arguments[0].shape[0]
-        head_dev = arguments[2].shape[1] // HD
-        shared = (H // KV) % (2 * head_dev) == 0
-        whole = ranks == 8 and groups == 4 and rows == BLOCK and shared
-        return (everywhere if whole else by_request)(*arguments)
+        rows, head_dev = arguments[0].shape[0], arguments[2].shape[1] // HD
+        if not gathers_all(mesh, rows, head_dev):
+            return by_request(*arguments)
+        return everywhere(*arguments)
 
     return jax.shard_map(
         per_device, mesh=mesh, in_specs=in_specs, out_specs=out_specs, check_vma=False

time: 24.4 us -> 24.5 us (level)
    pallas_call x1, Pallas kernels: 0.73 us -> 1.06 us  [everywhere(): pl.pallas_call(functools.partial(middle_kernel, columns(1, later)), out_s...]
  transfers between devices with their start and end apart: 10 -> 10, of which waited for: 5 -> 5; matrix products, arithmetic and copies ran while one was open for 1% -> 1% of each run, Pallas kernels for 18% -> 20%
where the time goes in v4:
time: 24.5 us; the launch traced here: 24.3 us
  starting transfers between devices  11.9 us (49%)
  Pallas kernels  6.53 us (27%)
  waiting for transfers between devices  5.42 us (22%)
  other arithmetic  0.32 us (1%)
    ppermute x10, starting transfers between devices, move(): return lax.ppermute(array, ('seq', 'head'), pairs)  11.9 us
    ppermute x10, waiting for transfers between devices, move(): return lax.ppermute(array, ('seq', 'head'), pairs)  5.42 us
    pallas_call x1, Pallas kernels, everywhere(): pl.pallas_call(functools.partial(load_kernel, H // KV // head_dev), out_s...  2.07 us
    pallas_call x1, Pallas kernels, everywhere(): pl.pallas_call(functools.partial(query_kernel, offsets), out_shape=(pltpu...  1.62 us
    pallas_call x1, Pallas kernels, everywhere(): pl.pallas_call(functools.partial(last_kernel, columns(later, ranks)), out...  1.2 us
    pallas_call x1, Pallas kernels, everywhere(): pl.pallas_call(functools.partial(middle_kernel, columns(1, later)), out_s...  1.06 us
    pallas_call x1, Pallas kernels, everywhere(): pl.pallas_call(kv_kernel, out_shape=(pltpu.VMEM((rows, 2 * HD), jnp.bfloa...  0.49 us
  transfers between devices with their start and end apart: 10, of which 5 were waited for; matrix products, arithmetic and copies ran while one was open for 1% of the time, Pallas kernels for 20%

profile of v4, /device:TPU:0, one launch (start us, length us, event | category | flops | bytes accessed | tf_op | source)
XLA Modules:
  0.0 24.3 jit_solution(11408208262124084500)
XLA Ops:
  0.0 3.0 %collective-permute-start.1 = (bf16[128,512]{1,0:T(8,128)(2,1)}, bf16[128,512]{1,0:T(8,128)(2,1)S(1)}, u32[]{:S(2)}, u32[]{:S(2)}) collective-permute-start(bf16[128,512]{1,0:T(8,128)(2,1)} %tokens.1), channel_id=1, source_target_pairs={{0,2},{1,3},{2,0},{3,1},{4,6},{5,7},{6,4},{7,5},{8,10},{9,11},{10,... | collective-permute-start | bytes 393224 | tf_op jit(solution)/shard_map/ppermute | solution.py:376
  3.0 0.0 collective-permute-start
  3.0 2.1 %load.1 = (bf16[128,512]{1,0:T(8,128)(2,1)S(1)}, f32[1,2048]{1,0:T(1,128)S(1)}, bf16[2048,256]{1,0:T(8,128)(2,1)S(1)}, bf16[2048,512]{1,0:T(8,128)(2,1)S(1)}, s32[1,128]{1,0:T(1,128)S(1)}) custom-call(bf16[128,512]{1,0:T(8,128)(2,1)} %tokens.1, f32[1,2048]{1,0:T(1,128)} %bitcast.2, bf16[2048,256]{1,0:T(8,128)(2,1)} %key_weight.1, ...), custom_call_target="tpu_custom_call" | custom-call | tf_op jit(solution)/shard_map/load/pallas_call | solution.py:381
  5.1 0.0 copy-start
  5.1 0.0 copy-start.1
  5.1 1.6 %collective-permute-done.1.refs_2_.x2 = bf16[128,512]{1,0:T(8,128)(2,1)S(1)} collective-permute-done((bf16[128,512]{1,0:T(8,128)(2,1)}, bf16[128,512]{1,0:T(8,128)(2,1)S(1)}, u32[]{:S(2)}, u32[]{:S(2)}) %collective-permute-start.1) | collective-permute-done | bytes 131104 | tf_op jit(solution)/shard_map/ppermute | solution.py:376
  6.7 0.0 collective-permute-start.2
  6.7 0.3 %multiply_sine_fusion = (f32[128,64]{1,0:T(8,128)S(1)}, f32[128,64]{1,0:T(8,128)S(1)}) fusion(f32[64]{0:T(128)S(1)} %multiply_power_fusion, f32[128]{0:T(128)S(1)} %add_convert_fusion), kind=kLoop, calls=%fused_computation | loop fusion | flops 8192 | bytes 66304 | tf_op jit(solution)/shard_map/sin | solution.py:412
  7.0 0.0 collective-permute-done.refs_1_.x1
  7.0 0.1 squares.1
  7.1 0.9 %collective-permute-done.2.x3 = bf16[128,512]{1,0:T(8,128)(2,1)S(1)} collective-permute-done((bf16[128,512]{1,0:T(8,128)(2,1)S(1)}, bf16[128,512]{1,0:T(8,128)(2,1)S(1)}, u32[]{:S(2)}, u32[]{:S(2)}) %collective-permute-start.2) | collective-permute-done | bytes 131104 | tf_op jit(solution)/shard_map/ppermute | solution.py:376
  8.0 0.5 %keys_values.1 = (bf16[128,256]{1,0:T(8,128)(2,1)S(1)}, bf16[128,2048]{1,0:T(8,128)(2,1)S(1)}) custom-call(f32[128,128]{1,0:T(8,128)S(1)} %squares.1, bf16[128,512]{1,0:T(8,128)(2,1)S(1)} %get-tuple-element.20.refs_0_.x0, bf16[128,512]{1,0:T(8,128)(2,1)S(1)} %collective-permute-done.refs_1_.x1, bf16[128,512]{1,0:T(8,128)(2,1)S(1)} %collective-permute-done.1.refs_2_.x2, ...), custom_call_target="tpu_custom_call" | custom-call | tf_op jit(solution)/shard_map/keys_values/pallas_call | solution.py:423
  8.5 2.9 %collective-permute-start.5 = (bf16[128,256]{1,0:T(8,128)(2,1)S(1)}, bf16[128,256]{1,0:T(8,128)(2,1)S(1)}, u32[]{:S(2)}, u32[]{:S(2)}) collective-permute-start(bf16[128,256]{1,0:T(8,128)(2,1)S(1)} %get-tuple-element.26.own), channel_id=1, source_target_pairs={{0,16},{1,25},{2,18},{3,27},{4,20},{5,29},{6,22},{7,31},{8,24},{9,... | collective-permute-start | bytes 196616 | tf_op jit(solution)/shard_map/ppermute | solution.py:376
  11.4 1.6 %collective-permute-start.3 = (bf16[128,256]{1,0:T(8,128)(2,1)S(1)}, bf16[128,256]{1,0:T(8,128)(2,1)S(1)}, u32[]{:S(2)}, u32[]{:S(2)}) collective-permute-start(bf16[128,256]{1,0:T(8,128)(2,1)S(1)} %get-tuple-element.26.own), channel_id=1, source_target_pairs={{0,8},{1,5},{2,10},{3,7},{4,12},{5,1},{6,14},{7,3},{8,0},{9,13},{1... | collective-permute-start | bytes 196616 | tf_op jit(solution)/shard_map/ppermute | solution.py:376
  13.0 1.3 %collective-permute-start.7 = (bf16[128,256]{1,0:T(8,128)(2,1)S(1)}, bf16[128,256]{1,0:T(8,128)(2,1)S(1)}, u32[]{:S(2)}, u32[]{:S(2)}) collective-permute-start(bf16[128,256]{1,0:T(8,128)(2,1)S(1)} %get-tuple-element.26.own), channel_id=1, source_target_pairs={{0,20},{1,29},{2,22},{3,31},{4,16},{5,25},{6,18},{7,27},{8,28},{9,... | collective-permute-start | bytes 196616 | tf_op jit(solution)/shard_map/ppermute | solution.py:376
  14.3 1.5 %collective-permute-done.5.refs_5_ = bf16[128,256]{1,0:T(8,128)(2,1)S(1)} collective-permute-done((bf16[128,256]{1,0:T(8,128)(2,1)S(1)}, bf16[128,256]{1,0:T(8,128)(2,1)S(1)}, u32[]{:S(2)}, u32[]{:S(2)}) %collective-permute-start.5) | collective-permute-done | bytes 65568 | tf_op jit(solution)/shard_map/ppermute | solution.py:376
  15.7 0.0 collective-permute-start.6
  15.7 0.3 %collective-permute-done.3.refs_3_ = bf16[128,256]{1,0:T(8,128)(2,1)S(1)} collective-permute-done((bf16[128,256]{1,0:T(8,128)(2,1)S(1)}, bf16[128,256]{1,0:T(8,128)(2,1)S(1)}, u32[]{:S(2)}, u32[]{:S(2)}) %collective-permute-start.3) | collective-permute-done | bytes 65568 | tf_op jit(solution)/shard_map/ppermute | solution.py:376
  16.1 0.2 collective-permute-start.4
  16.2 3.0 %collective-permute-start.8 = (bf16[128,256]{1,0:T(8,128)(2,1)S(1)}, bf16[128,256]{1,0:T(8,128)(2,1)S(1)}, u32[]{:S(2)}, u32[]{:S(2)}) collective-permute-start(bf16[128,256]{1,0:T(8,128)(2,1)S(1)} %get-tuple-element.26.own), channel_id=1, source_target_pairs={{0,12},{1,13},{2,14},{3,15},{4,8},{5,9},{6,10},{7,11},{8,4},{9,5},... | collective-permute-start | bytes 196616 | tf_op jit(solution)/shard_map/ppermute | solution.py:376
  19.3 1.1 %collective-permute-done.7.refs_7_ = bf16[128,256]{1,0:T(8,128)(2,1)S(1)} collective-permute-done((bf16[128,256]{1,0:T(8,128)(2,1)S(1)}, bf16[128,256]{1,0:T(8,128)(2,1)S(1)}, u32[]{:S(2)}, u32[]{:S(2)}) %collective-permute-start.7) | collective-permute-done | bytes 65568 | tf_op jit(solution)/shard_map/ppermute | solution.py:376
  20.4 0.0 collective-permute-start.9
  20.4 0.0 copy-done
  20.4 0.0 copy-done.1
  20.4 1.6 %queries.1 = (bf16[512,128]{1,0:T(8,128)(2,1)S(1)}, f32[128,1024]{1,0:T(8,128)S(1)}, f32[512,128]{1,0:T(8,128)S(1)}, f32[512,128]{1,0:T(8,128)S(1)}, f32[512,128]{1,0:T(8,128)S(1)}) custom-call(s32[8]{0:T(128)S(1)} %copy-done, s32[1,2]{1,0:T(1,128)S(1)} %copy-done.1, bf16[128,2048]{1,0:T(8,128)(2,1)S(1)} %get-tuple-element.23.normed, ...), custom_call_target="tpu_custom_call" | custom-call | tf_op jit(solution)/shard_map/queries/pallas_call | solution.py:477
  22.0 0.0 collective-permute-done.6.refs_6_
  22.0 0.0 collective-permute-done.4.refs_4_
  22.0 1.1 %middle.1 = (f32[512,128]{1,0:T(8,128)S(1)}, f32[512,128]{1,0:T(8,128)S(1)}, f32[512,128]{1,0:T(8,128)S(1)}) custom-call(bf16[512,128]{1,0:T(8,128)(2,1)S(1)} %get-tuple-element.27.q, f32[128,1024]{1,0:T(8,128)S(1)} %get-tuple-element.28.bias, f32[512,128]{1,0:T(8,128)S(1)} %get-tuple-element.29.refs_0_, f32[512,128]{1,0:T(8,128)S(1)} %get-tuple-element.30.refs_1_, ...), custom_call_target="tpu_custom_call" | custom-call | tf_op jit(solution)/shard_map/middle/pallas_call | solution.py:504
  23.1 0.0 collective-permute-done.8.refs_3_
  23.1 0.0 collective-permute-done.9.refs_4_
  23.1 1.2 %last.1 = bf16[128,512]{1,0:T(8,128)(2,1)} custom-call(bf16[512,128]{1,0:T(8,128)(2,1)S(1)} %get-tuple-element.27.q, f32[128,1024]{1,0:T(8,128)S(1)} %get-tuple-element.28.bias, f32[512,128]{1,0:T(8,128)S(1)} %get-tuple-element.32.refs_0_, f32[512,128]{1,0:T(8,128)S(1)} %get-tuple-element.33.refs_1_, f32[512,128]{1,0:T(8,128)S(1)} %get-tuple-element.34.refs_2_, ...), custom_call_target="tpu_custom_call" | custom-call | tf_op jit(solution)/shard_map/last/pallas_call | solution.py:513
  (2 shorter events, 0.0 us)
Async XLA Ops:
  0.0 6.7 %collective-permute-start.1 = (bf16[128,512]{1,0:T(8,128)(2,1)}, bf16[128,512]{1,0:T(8,128)(2,1)S(1)}, u32[]{:S(2)}, u32[]{:S(2)}) collective-permute-start(bf16[128,512]{1,0:T(8,128)(2,1)} %tokens.1), channel_id=1, source_target_pairs={{0,2},{1,3},{2,0},{3,1},{4,6},{5,7},{6,4},{7,5},{8,10},{9,11},{10,... | collective-permute-start | bytes 393224 | tf_op jit(solution)/shard_map/ppermute | solution.py:376
  3.0 4.0 %collective-permute-start = (bf16[128,512]{1,0:T(8,128)(2,1)}, bf16[128,512]{1,0:T(8,128)(2,1)S(1)}, u32[]{:S(2)}, u32[]{:S(2)}) collective-permute-start(bf16[128,512]{1,0:T(8,128)(2,1)} %tokens.1), channel_id=1, source_target_pairs={{0,1},{1,0},{2,3},{3,2},{4,5},{5,4},{6,7},{7,6},{8,9},{9,8},{10,11... | collective-permute-start | bytes 393224 | tf_op jit(solution)/shard_map/ppermute | solution.py:376
  5.1 15.3 %copy-start = (s32[8]{0:T(128)S(1)}, s32[8]{0:T(128)}, u32[]{:S(2)}) copy-start(s32[8]{0:T(128)} %lengths.1) | copy-start | bytes 100
  5.1 15.3 %copy-start.1 = (s32[1,2]{1,0:T(1,128)S(1)}, s32[1,2]{1,0:T(1,128)}, u32[]{:S(2)}) copy-start(s32[1,2]{1,0:T(1,128)} %spans.1) | copy-start | bytes 28
  6.7 1.3 %collective-permute-start.2 = (bf16[128,512]{1,0:T(8,128)(2,1)S(1)}, bf16[128,512]{1,0:T(8,128)(2,1)S(1)}, u32[]{:S(2)}, u32[]{:S(2)}) collective-permute-start(bf16[128,512]{1,0:T(8,128)(2,1)S(1)} %collective-permute-done.1.refs_2_.x2), channel_id=1, source_target_pairs={{0,1},{1,0},{2,3},{3,2},{4,5},{5,4},{6,7},{7,6},{8,9},{9,8},{10,11... | collective-permute-start | bytes 393224 | tf_op jit(solution)/shard_map/ppermute | solution.py:376
  8.5 7.2 %collective-permute-start.5 = (bf16[128,256]{1,0:T(8,128)(2,1)S(1)}, bf16[128,256]{1,0:T(8,128)(2,1)S(1)}, u32[]{:S(2)}, u32[]{:S(2)}) collective-permute-start(bf16[128,256]{1,0:T(8,128)(2,1)S(1)} %get-tuple-element.26.own), channel_id=1, source_target_pairs={{0,16},{1,25},{2,18},{3,27},{4,20},{5,29},{6,22},{7,31},{8,24},{9,... | collective-permute-start | bytes 196616 | tf_op jit(solution)/shard_map/ppermute | solution.py:376
  11.4 4.6 %collective-permute-start.3 = (bf16[128,256]{1,0:T(8,128)(2,1)S(1)}, bf16[128,256]{1,0:T(8,128)(2,1)S(1)}, u32[]{:S(2)}, u32[]{:S(2)}) collective-permute-start(bf16[128,256]{1,0:T(8,128)(2,1)S(1)} %get-tuple-element.26.own), channel_id=1, source_target_pairs={{0,8},{1,5},{2,10},{3,7},{4,12},{5,1},{6,14},{7,3},{8,0},{9,13},{1... | collective-permute-start | bytes 196616 | tf_op jit(solution)/shard_map/ppermute | solution.py:376
  13.0 7.4 %collective-permute-start.7 = (bf16[128,256]{1,0:T(8,128)(2,1)S(1)}, bf16[128,256]{1,0:T(8,128)(2,1)S(1)}, u32[]{:S(2)}, u32[]{:S(2)}) collective-permute-start(bf16[128,256]{1,0:T(8,128)(2,1)S(1)} %get-tuple-element.26.own), channel_id=1, source_target_pairs={{0,20},{1,29},{2,22},{3,31},{4,16},{5,25},{6,18},{7,27},{8,28},{9,... | collective-permute-start | bytes 196616 | tf_op jit(solution)/shard_map/ppermute | solution.py:376
  15.7 6.3 %collective-permute-start.6 = (bf16[128,256]{1,0:T(8,128)(2,1)S(1)}, bf16[128,256]{1,0:T(8,128)(2,1)S(1)}, u32[]{:S(2)}, u32[]{:S(2)}) collective-permute-start(bf16[128,256]{1,0:T(8,128)(2,1)S(1)} %collective-permute-done.5.refs_5_), channel_id=1, source_target_pairs={{0,1},{1,0},{2,3},{3,2},{4,5},{5,4},{6,7},{7,6},{8,9},{9,8},{10,11... | collective-permute-start | bytes 196616 | tf_op jit(solution)/shard_map/ppermute | solution.py:376
  16.1 6.0 %collective-permute-start.4 = (bf16[128,256]{1,0:T(8,128)(2,1)S(1)}, bf16[128,256]{1,0:T(8,128)(2,1)S(1)}, u32[]{:S(2)}, u32[]{:S(2)}) collective-permute-start(bf16[128,256]{1,0:T(8,128)(2,1)S(1)} %collective-permute-done.3.refs_3_), channel_id=1, source_target_pairs={{0,1},{1,0},{2,3},{3,2},{4,5},{5,4},{6,7},{7,6},{8,9},{9,8},{10,11... | collective-permute-start | bytes 196616 | tf_op jit(solution)/shard_map/ppermute | solution.py:376
  16.2 6.9 %collective-permute-start.8 = (bf16[128,256]{1,0:T(8,128)(2,1)S(1)}, bf16[128,256]{1,0:T(8,128)(2,1)S(1)}, u32[]{:S(2)}, u32[]{:S(2)}) collective-permute-start(bf16[128,256]{1,0:T(8,128)(2,1)S(1)} %get-tuple-element.26.own), channel_id=1, source_target_pairs={{0,12},{1,13},{2,14},{3,15},{4,8},{5,9},{6,10},{7,11},{8,4},{9,5},... | collective-permute-start | bytes 196616 | tf_op jit(solution)/shard_map/ppermute | solution.py:376
  20.4 2.7 %collective-permute-start.9 = (bf16[128,256]{1,0:T(8,128)(2,1)S(1)}, bf16[128,256]{1,0:T(8,128)(2,1)S(1)}, u32[]{:S(2)}, u32[]{:S(2)}) collective-permute-start(bf16[128,256]{1,0:T(8,128)(2,1)S(1)} %collective-permute-done.7.refs_7_), channel_id=1, source_target_pairs={{0,1},{1,0},{2,3},{3,2},{4,5},{5,4},{6,7},{7,6},{8,9},{9,8},{10,11... | collective-permute-start | bytes 196616 | tf_op jit(solution)/shard_map/ppermute | solution.py:376

commit v5 on v4

--- a/solution.py
+++ b/solution.py
@@ -451,19 +451,19 @@
     def split(array, both):
         return move(array, lambda g: (both[g % 2], 0))
 
-    column = split(key_values, (far, far | 2))
-    row = split(key_values, (2, 1))
+    column = split(key_values, (far, 2))
+    diagonal = split(key_values, (far | 2, far | 1))
+    row = split(key_values, (1, far | 3))
     corner = split(key_values, (3, 3))
-    diagonal = split(key_values, (far | 1, far | 3))
     held = [
         ((0, 0), key_values),
-        ((2, 1), row),
-        ((1, 2), swapped(row)),
-        ((far, far | 2), column),
-        ((far | 2, far), swapped(column)),
-        ((far | 1, far | 3), diagonal),
+        ((far, 2), column),
+        ((2, far), swapped(column)),
+        ((far | 2, far | 1), diagonal),
+        ((far | 1, far | 2), swapped(diagonal)),
+        ((1, far | 3), row),
         ((3, 3), corner),
-        ((far | 3, far | 1), swapped(diagonal)),
+        ((far | 3, 1), swapped(row)),
     ]
     offsets, arrays = [offset for offset, _ in held], [near_core(array) for _, array in held]
     state = [pltpu.VMEM((tall, BLOCK), jnp.float32)] * 2 + [pltpu.VMEM((tall, HD), jnp.float32)]
@@ -500,16 +500,16 @@
     def columns(first, end):
         return [order * BLOCK for order in range(first, end)]
 
-    later = ranks - 2
-    partial = pl.pallas_call(
-        functools.partial(middle_kernel, columns(1, later)),
-        out_shape=tuple(state),
-        in_specs=vmem(5 + later - 1),
-        out_specs=tuple(vmem(3)),
-        scratch_shapes=work(later - 1),
-        compiler_params=grant(6),
-        name="middle",
-    )(*[near_core(array) for array in (q, bias, *partial)], *arrays[1:later])
+    early, later = ranks // 2, ranks - 2
+    for first, end in ((1, early), (early, later)):
+        partial = pl.pallas_call(
+            functools.partial(middle_kernel, columns(first, end)),
+            out_shape=tuple(state),
+            in_specs=vmem(5 + end - first),
+            out_specs=tuple(vmem(3)),
+            scratch_shapes=work(end - first),
+            compiler_params=grant(6),
+        )(*[near_core(array) for array in (q, bias, *partial)], *arrays[first:end])
     return pl.pallas_call(
         functools.partial(last_kernel, columns(later, ranks)),
         out_shape=jax.ShapeDtypeStruct((rows, head_dev * HD), jnp.bfloat16),

time: 24.5 us -> 24.7 us (level)
  waiting for transfers between devices: 5.42 us -> 5.85 us
    ppermute x10, waiting for transfers between devices: 5.42 us -> 5.85 us  [move(): return lax.ppermute(array, ('seq', 'head'), pairs)]
    ppermute x10, starting transfers between devices: 11.9 us -> 11.7 us  [move(): return lax.ppermute(array, ('seq', 'head'), pairs)]
    pallas_call x1 -> x2, Pallas kernels: 1.06 us -> 1.15 us  [everywhere(): pl.pallas_call(functools.partial(middle_kernel, columns(first, end)), out...]
  transfers between devices with their start and end apart: 10 -> 10, of which waited for: 5 -> 3; matrix products, arithmetic and copies ran while one was open for 1% -> 1% of each run, Pallas kernels for 20% -> 20%
where the time goes in v5:
time: 24.7 us; the launch traced here: 24.6 us
  starting transfers between devices  11.7 us (47%)
  Pallas kernels  6.62 us (27%)
  waiting for transfers between devices  5.85 us (24%)
  other arithmetic  0.32 us (1%)
    ppermute x10, starting transfers between devices, move(): return lax.ppermute(array, ('seq', 'head'), pairs)  11.7 us
    ppermute x10, waiting for transfers between devices, move(): return lax.ppermute(array, ('seq', 'head'), pairs)  5.85 us
    pallas_call x1, Pallas kernels, everywhere(): pl.pallas_call(functools.partial(load_kernel, H // KV // head_dev), out_s...  2.07 us
    pallas_call x1, Pallas kernels, everywhere(): pl.pallas_call(functools.partial(query_kernel, offsets), out_shape=(pltpu...  1.62 us
    pallas_call x1, Pallas kernels, everywhere(): pl.pallas_call(functools.partial(last_kernel, columns(later, ranks)), out...  1.2 us
    pallas_call x2, Pallas kernels, everywhere(): pl.pallas_call(functools.partial(middle_kernel, columns(first, end)), out...  1.15 us
  transfers between devices with their start and end apart: 10, of which 3 were waited for; matrix products, arithmetic and copies ran while one was open for 1% of the time, Pallas kernels for 20%

profile of v5, /device:TPU:0, one launch (start us, length us, event | category | flops | bytes accessed | tf_op | source)
XLA Modules:
  0.0 24.6 jit_solution(3239248700053843654)
XLA Ops:
  0.0 3.0 %collective-permute-start.1 = (bf16[128,512]{1,0:T(8,128)(2,1)}, bf16[128,512]{1,0:T(8,128)(2,1)S(1)}, u32[]{:S(2)}, u32[]{:S(2)}) collective-permute-start(bf16[128,512]{1,0:T(8,128)(2,1)} %tokens.1), channel_id=1, source_target_pairs={{0,2},{1,3},{2,0},{3,1},{4,6},{5,7},{6,4},{7,5},{8,10},{9,11},{10,... | collective-permute-start | bytes 393224 | tf_op jit(solution)/shard_map/ppermute | solution.py:376
  3.0 0.0 collective-permute-start
  3.0 2.1 %load.1 = (bf16[128,512]{1,0:T(8,128)(2,1)S(1)}, f32[1,2048]{1,0:T(1,128)S(1)}, bf16[2048,256]{1,0:T(8,128)(2,1)S(1)}, bf16[2048,512]{1,0:T(8,128)(2,1)S(1)}, s32[1,128]{1,0:T(1,128)S(1)}) custom-call(bf16[128,512]{1,0:T(8,128)(2,1)} %tokens.1, f32[1,2048]{1,0:T(1,128)} %bitcast.2, bf16[2048,256]{1,0:T(8,128)(2,1)} %key_weight.1, ...), custom_call_target="tpu_custom_call" | custom-call | tf_op jit(solution)/shard_map/load/pallas_call | solution.py:381
  5.1 0.0 copy-start
  5.1 0.0 copy-start.1
  5.1 1.6 %collective-permute-done.1.refs_2_.x2 = bf16[128,512]{1,0:T(8,128)(2,1)S(1)} collective-permute-done((bf16[128,512]{1,0:T(8,128)(2,1)}, bf16[128,512]{1,0:T(8,128)(2,1)S(1)}, u32[]{:S(2)}, u32[]{:S(2)}) %collective-permute-start.1) | collective-permute-done | bytes 131104 | tf_op jit(solution)/shard_map/ppermute | solution.py:376
  6.7 0.0 collective-permute-start.2
  6.7 0.3 %multiply_sine_fusion = (f32[128,64]{1,0:T(8,128)S(1)}, f32[128,64]{1,0:T(8,128)S(1)}) fusion(f32[64]{0:T(128)S(1)} %multiply_power_fusion, f32[128]{0:T(128)S(1)} %add_convert_fusion), kind=kLoop, calls=%fused_computation | loop fusion | flops 8192 | bytes 66304 | tf_op jit(solution)/shard_map/sin | solution.py:412
  7.0 0.0 collective-permute-done.refs_1_.x1
  7.0 0.1 squares.1
  7.1 0.9 %collective-permute-done.2.x3 = bf16[128,512]{1,0:T(8,128)(2,1)S(1)} collective-permute-done((bf16[128,512]{1,0:T(8,128)(2,1)S(1)}, bf16[128,512]{1,0:T(8,128)(2,1)S(1)}, u32[]{:S(2)}, u32[]{:S(2)}) %collective-permute-start.2) | collective-permute-done | bytes 131104 | tf_op jit(solution)/shard_map/ppermute | solution.py:376
  8.0 0.5 %keys_values.1 = (bf16[128,256]{1,0:T(8,128)(2,1)S(1)}, bf16[128,2048]{1,0:T(8,128)(2,1)S(1)}) custom-call(f32[128,128]{1,0:T(8,128)S(1)} %squares.1, bf16[128,512]{1,0:T(8,128)(2,1)S(1)} %get-tuple-element.23.refs_0_.x0, bf16[128,512]{1,0:T(8,128)(2,1)S(1)} %collective-permute-done.refs_1_.x1, bf16[128,512]{1,0:T(8,128)(2,1)S(1)} %collective-permute-done.1.refs_2_.x2, ...), custom_call_target="tpu_custom_call" | custom-call | tf_op jit(solution)/shard_map/keys_values/pallas_call | solution.py:423
  8.5 2.9 %collective-permute-start.3 = (bf16[128,256]{1,0:T(8,128)(2,1)S(1)}, bf16[128,256]{1,0:T(8,128)(2,1)S(1)}, u32[]{:S(2)}, u32[]{:S(2)}) collective-permute-start(bf16[128,256]{1,0:T(8,128)(2,1)S(1)} %get-tuple-element.29.own), channel_id=1, source_target_pairs={{0,16},{1,9},{2,18},{3,11},{4,20},{5,13},{6,22},{7,15},{8,24},{9,1... | collective-permute-start | bytes 196616 | tf_op jit(solution)/shard_map/ppermute | solution.py:376
  11.4 1.3 %collective-permute-start.5 = (bf16[128,256]{1,0:T(8,128)(2,1)S(1)}, bf16[128,256]{1,0:T(8,128)(2,1)S(1)}, u32[]{:S(2)}, u32[]{:S(2)}) collective-permute-start(bf16[128,256]{1,0:T(8,128)(2,1)S(1)} %get-tuple-element.29.own), channel_id=1, source_target_pairs={{0,24},{1,21},{2,26},{3,23},{4,28},{5,17},{6,30},{7,19},{8,16},{9,... | collective-permute-start | bytes 196616 | tf_op jit(solution)/shard_map/ppermute | solution.py:376
  12.8 1.5 %collective-permute-start.7 = (bf16[128,256]{1,0:T(8,128)(2,1)S(1)}, bf16[128,256]{1,0:T(8,128)(2,1)S(1)}, u32[]{:S(2)}, u32[]{:S(2)}) collective-permute-start(bf16[128,256]{1,0:T(8,128)(2,1)S(1)} %get-tuple-element.29.own), channel_id=1, source_target_pairs={{0,4},{1,29},{2,6},{3,31},{4,0},{5,25},{6,2},{7,27},{8,12},{9,21},... | collective-permute-start | bytes 196616 | tf_op jit(solution)/shard_map/ppermute | solution.py:376
  14.3 0.0 collective-permute-done.3.refs_3_
  14.3 0.0 collective-permute-start.4
  14.3 3.3 %collective-permute-done.5.refs_5_ = bf16[128,256]{1,0:T(8,128)(2,1)S(1)} collective-permute-done((bf16[128,256]{1,0:T(8,128)(2,1)S(1)}, bf16[128,256]{1,0:T(8,128)(2,1)S(1)}, u32[]{:S(2)}, u32[]{:S(2)}) %collective-permute-start.5) | collective-permute-done | bytes 65568 | tf_op jit(solution)/shard_map/ppermute | solution.py:376
  17.6 0.0 collective-permute-start.6
  17.6 2.7 %collective-permute-start.8 = (bf16[128,256]{1,0:T(8,128)(2,1)S(1)}, bf16[128,256]{1,0:T(8,128)(2,1)S(1)}, u32[]{:S(2)}, u32[]{:S(2)}) collective-permute-start(bf16[128,256]{1,0:T(8,128)(2,1)S(1)} %get-tuple-element.29.own), channel_id=1, source_target_pairs={{0,12},{1,13},{2,14},{3,15},{4,8},{5,9},{6,10},{7,11},{8,4},{9,5},... | collective-permute-start | bytes 196616 | tf_op jit(solution)/shard_map/ppermute | solution.py:376
  20.3 0.0 collective-permute-done.7.refs_4_
  20.3 0.2 collective-permute-start.9
  20.5 0.0 copy-done
  20.5 0.0 copy-done.1
  20.5 1.6 %queries.1 = (bf16[512,128]{1,0:T(8,128)(2,1)S(1)}, f32[128,1024]{1,0:T(8,128)S(1)}, f32[512,128]{1,0:T(8,128)S(1)}, f32[512,128]{1,0:T(8,128)S(1)}, f32[512,128]{1,0:T(8,128)S(1)}) custom-call(s32[8]{0:T(128)S(1)} %copy-done, s32[1,2]{1,0:T(1,128)S(1)} %copy-done.1, bf16[128,2048]{1,0:T(8,128)(2,1)S(1)} %get-tuple-element.26.normed, ...), custom_call_target="tpu_custom_call" | custom-call | tf_op jit(solution)/shard_map/queries/pallas_call | solution.py:477
  22.2 0.0 collective-permute-done.4.refs_4_
  22.2 0.6 %shard_map.82 = (f32[512,128]{1,0:T(8,128)S(1)}, f32[512,128]{1,0:T(8,128)S(1)}, f32[512,128]{1,0:T(8,128)S(1)}) custom-call(bf16[512,128]{1,0:T(8,128)(2,1)S(1)} %get-tuple-element.30.q, f32[128,1024]{1,0:T(8,128)S(1)} %get-tuple-element.31.bias, f32[512,128]{1,0:T(8,128)S(1)} %get-tuple-element.32.refs_0_, f32[512,128]{1,0:T(8,128)S(1)} %get-tuple-element.33.refs_1_, ...), custom_call_target="tpu_custom_call" | custom-call | tf_op jit(solution)/shard_map/pallas_call | solution.py:505
  22.8 0.0 collective-permute-done.6.refs_3_
  22.8 0.5 %shard_map.83 = (f32[512,128]{1,0:T(8,128)S(1)}, f32[512,128]{1,0:T(8,128)S(1)}, f32[512,128]{1,0:T(8,128)S(1)}) custom-call(bf16[512,128]{1,0:T(8,128)(2,1)S(1)} %get-tuple-element.30.q, f32[128,1024]{1,0:T(8,128)S(1)} %get-tuple-element.31.bias, f32[512,128]{1,0:T(8,128)S(1)} %get-tuple-element.35.refs_0_, f32[512,128]{1,0:T(8,128)S(1)} %get-tuple-element.36.refs_1_, ...), custom_call_target="tpu_custom_call" | custom-call | tf_op jit(solution)/shard_map/pallas_call | solution.py:505
  23.3 0.0 collective-permute-done.8.refs_3_
  23.4 0.0 collective-permute-done.9.refs_4_
  23.4 1.2 %last.1 = bf16[128,512]{1,0:T(8,128)(2,1)} custom-call(bf16[512,128]{1,0:T(8,128)(2,1)S(1)} %get-tuple-element.30.q, f32[128,1024]{1,0:T(8,128)S(1)} %get-tuple-element.31.bias, f32[512,128]{1,0:T(8,128)S(1)} %get-tuple-element.38.refs_0_, f32[512,128]{1,0:T(8,128)S(1)} %get-tuple-element.39.refs_1_, f32[512,128]{1,0:T(8,128)S(1)} %get-tuple-element.40.refs_2_, ...), custom_call_target="tpu_custom_call" | custom-call | tf_op jit(solution)/shard_map/last/pallas_call | solution.py:513
  (2 shorter events, 0.0 us)
Async XLA Ops:
  0.0 6.7 %collective-permute-start.1 = (bf16[128,512]{1,0:T(8,128)(2,1)}, bf16[128,512]{1,0:T(8,128)(2,1)S(1)}, u32[]{:S(2)}, u32[]{:S(2)}) collective-permute-start(bf16[128,512]{1,0:T(8,128)(2,1)} %tokens.1), channel_id=1, source_target_pairs={{0,2},{1,3},{2,0},{3,1},{4,6},{5,7},{6,4},{7,5},{8,10},{9,11},{10,... | collective-permute-start | bytes 393224 | tf_op jit(solution)/shard_map/ppermute | solution.py:376
  3.0 4.0 %collective-permute-start = (bf16[128,512]{1,0:T(8,128)(2,1)}, bf16[128,512]{1,0:T(8,128)(2,1)S(1)}, u32[]{:S(2)}, u32[]{:S(2)}) collective-permute-start(bf16[128,512]{1,0:T(8,128)(2,1)} %tokens.1), channel_id=1, source_target_pairs={{0,1},{1,0},{2,3},{3,2},{4,5},{5,4},{6,7},{7,6},{8,9},{9,8},{10,11... | collective-permute-start | bytes 393224 | tf_op jit(solution)/shard_map/ppermute | solution.py:376
  5.1 15.4 %copy-start = (s32[8]{0:T(128)S(1)}, s32[8]{0:T(128)}, u32[]{:S(2)}) copy-start(s32[8]{0:T(128)} %lengths.1) | copy-start | bytes 100
  5.1 15.4 %copy-start.1 = (s32[1,2]{1,0:T(1,128)S(1)}, s32[1,2]{1,0:T(1,128)}, u32[]{:S(2)}) copy-start(s32[1,2]{1,0:T(1,128)} %spans.1) | copy-start | bytes 28
  6.7 1.3 %collective-permute-start.2 = (bf16[128,512]{1,0:T(8,128)(2,1)S(1)}, bf16[128,512]{1,0:T(8,128)(2,1)S(1)}, u32[]{:S(2)}, u32[]{:S(2)}) collective-permute-start(bf16[128,512]{1,0:T(8,128)(2,1)S(1)} %collective-permute-done.1.refs_2_.x2), channel_id=1, source_target_pairs={{0,1},{1,0},{2,3},{3,2},{4,5},{5,4},{6,7},{7,6},{8,9},{9,8},{10,11... | collective-permute-start | bytes 393224 | tf_op jit(solution)/shard_map/ppermute | solution.py:376
  8.5 5.7 %collective-permute-start.3 = (bf16[128,256]{1,0:T(8,128)(2,1)S(1)}, bf16[128,256]{1,0:T(8,128)(2,1)S(1)}, u32[]{:S(2)}, u32[]{:S(2)}) collective-permute-start(bf16[128,256]{1,0:T(8,128)(2,1)S(1)} %get-tuple-element.29.own), channel_id=1, source_target_pairs={{0,16},{1,9},{2,18},{3,11},{4,20},{5,13},{6,22},{7,15},{8,24},{9,1... | collective-permute-start | bytes 196616 | tf_op jit(solution)/shard_map/ppermute | solution.py:376
  11.4 6.2 %collective-permute-start.5 = (bf16[128,256]{1,0:T(8,128)(2,1)S(1)}, bf16[128,256]{1,0:T(8,128)(2,1)S(1)}, u32[]{:S(2)}, u32[]{:S(2)}) collective-permute-start(bf16[128,256]{1,0:T(8,128)(2,1)S(1)} %get-tuple-element.29.own), channel_id=1, source_target_pairs={{0,24},{1,21},{2,26},{3,23},{4,28},{5,17},{6,30},{7,19},{8,16},{9,... | collective-permute-start | bytes 196616 | tf_op jit(solution)/shard_map/ppermute | solution.py:376
  12.8 7.5 %collective-permute-start.7 = (bf16[128,256]{1,0:T(8,128)(2,1)S(1)}, bf16[128,256]{1,0:T(8,128)(2,1)S(1)}, u32[]{:S(2)}, u32[]{:S(2)}) collective-permute-start(bf16[128,256]{1,0:T(8,128)(2,1)S(1)} %get-tuple-element.29.own), channel_id=1, source_target_pairs={{0,4},{1,29},{2,6},{3,31},{4,0},{5,25},{6,2},{7,27},{8,12},{9,21},... | collective-permute-start | bytes 196616 | tf_op jit(solution)/shard_map/ppermute | solution.py:376
  14.3 7.9 %collective-permute-start.4 = (bf16[128,256]{1,0:T(8,128)(2,1)S(1)}, bf16[128,256]{1,0:T(8,128)(2,1)S(1)}, u32[]{:S(2)}, u32[]{:S(2)}) collective-permute-start(bf16[128,256]{1,0:T(8,128)(2,1)S(1)} %collective-permute-done.3.refs_3_), channel_id=1, source_target_pairs={{0,1},{1,0},{2,3},{3,2},{4,5},{5,4},{6,7},{7,6},{8,9},{9,8},{10,11... | collective-permute-start | bytes 196616 | tf_op jit(solution)/shard_map/ppermute | solution.py:376
  17.6 5.2 %collective-permute-start.6 = (bf16[128,256]{1,0:T(8,128)(2,1)S(1)}, bf16[128,256]{1,0:T(8,128)(2,1)S(1)}, u32[]{:S(2)}, u32[]{:S(2)}) collective-permute-start(bf16[128,256]{1,0:T(8,128)(2,1)S(1)} %collective-permute-done.5.refs_5_), channel_id=1, source_target_pairs={{0,1},{1,0},{2,3},{3,2},{4,5},{5,4},{6,7},{7,6},{8,9},{9,8},{10,11... | collective-permute-start | bytes 196616 | tf_op jit(solution)/shard_map/ppermute | solution.py:376
  17.6 5.8 %collective-permute-start.8 = (bf16[128,256]{1,0:T(8,128)(2,1)S(1)}, bf16[128,256]{1,0:T(8,128)(2,1)S(1)}, u32[]{:S(2)}, u32[]{:S(2)}) collective-permute-start(bf16[128,256]{1,0:T(8,128)(2,1)S(1)} %get-tuple-element.29.own), channel_id=1, source_target_pairs={{0,12},{1,13},{2,14},{3,15},{4,8},{5,9},{6,10},{7,11},{8,4},{9,5},... | collective-permute-start | bytes 196616 | tf_op jit(solution)/shard_map/ppermute | solution.py:376
  20.3 3.1 %collective-permute-start.9 = (bf16[128,256]{1,0:T(8,128)(2,1)S(1)}, bf16[128,256]{1,0:T(8,128)(2,1)S(1)}, u32[]{:S(2)}, u32[]{:S(2)}) collective-permute-start(bf16[128,256]{1,0:T(8,128)(2,1)S(1)} %collective-permute-done.7.refs_4_), channel_id=1, source_target_pairs={{0,1},{1,0},{2,3},{3,2},{4,5},{5,4},{6,7},{7,6},{8,9},{9,8},{10,11... | collective-permute-start | bytes 196616 | tf_op jit(solution)/shard_map/ppermute | solution.py:376

commit v6 on v5

--- a/solution.py
+++ b/solution.py
@@ -451,19 +451,19 @@
     def split(array, both):
         return move(array, lambda g: (both[g % 2], 0))
 
-    column = split(key_values, (far, 2))
-    diagonal = split(key_values, (far | 2, far | 1))
-    row = split(key_values, (1, far | 3))
+    column = split(key_values, (far, far | 2))
+    row = split(key_values, (1, 2))
     corner = split(key_values, (3, 3))
+    diagonal = split(key_values, (far | 1, far | 3))
     held = [
         ((0, 0), key_values),
-        ((far, 2), column),
-        ((2, far), swapped(column)),
-        ((far | 2, far | 1), diagonal),
-        ((far | 1, far | 2), swapped(diagonal)),
-        ((1, far | 3), row),
+        ((1, 2), row),
+        ((far, far | 2), column),
+        ((2, 1), swapped(row)),
+        ((far | 2, far), swapped(column)),
+        ((far | 1, far | 3), diagonal),
         ((3, 3), corner),
-        ((far | 3, 1), swapped(row)),
+        ((far | 3, far | 1), swapped(diagonal)),
     ]
     offsets, arrays = [offset for offset, _ in held], [near_core(array) for _, array in held]
     state = [pltpu.VMEM((tall, BLOCK), jnp.float32)] * 2 + [pltpu.VMEM((tall, HD), jnp.float32)]
@@ -500,7 +500,7 @@
     def columns(first, end):
         return [order * BLOCK for order in range(first, end)]
 
-    early, later = ranks // 2, ranks - 2
+    early, later = 3, ranks - 2
     for first, end in ((1, early), (early, later)):
         partial = pl.pallas_call(
             functools.partial(middle_kernel, columns(first, end)),

time: 24.7 us -> 23.8 us (0.964)
  waiting for transfers between devices: 5.85 us -> 5.22 us
  starting transfers between devices: 11.7 us -> 11.2 us
    ppermute x10, waiting for transfers between devices: 5.85 us -> 5.22 us  [move(): return lax.ppermute(array, ('seq', 'head'), pairs)]
    ppermute x10, starting transfers between devices: 11.7 us -> 11.2 us  [move(): return lax.ppermute(array, ('seq', 'head'), pairs)]
  transfers between devices with their start and end apart: 10 -> 10, of which waited for: 3 -> 4; matrix products, arithmetic and copies ran while one was open for 1% -> 1% of each run, Pallas kernels for 20% -> 21%
where the time goes in v6:
time: 23.8 us; the launch traced here: 23.5 us
  starting transfers between devices  11.2 us (47%)
  Pallas kernels  6.62 us (28%)
  waiting for transfers between devices  5.22 us (22%)
  other arithmetic  0.32 us (1%)
    ppermute x10, starting transfers between devices, move(): return lax.ppermute(array, ('seq', 'head'), pairs)  11.2 us
    ppermute x10, waiting for transfers between devices, move(): return lax.ppermute(array, ('seq', 'head'), pairs)  5.22 us
    pallas_call x1, Pallas kernels, everywhere(): pl.pallas_call(functools.partial(load_kernel, H // KV // head_dev), out_s...  2.07 us
    pallas_call x1, Pallas kernels, everywhere(): pl.pallas_call(functools.partial(query_kernel, offsets), out_shape=(pltpu...  1.62 us
    pallas_call x1, Pallas kernels, everywhere(): pl.pallas_call(functools.partial(last_kernel, columns(later, ranks)), out...  1.2 us
    pallas_call x2, Pallas kernels, everywhere(): pl.pallas_call(functools.partial(middle_kernel, columns(first, end)), out...  1.15 us
    pallas_call x1, Pallas kernels, everywhere(): pl.pallas_call(kv_kernel, out_shape=(pltpu.VMEM((rows, 2 * HD), jnp.bfloa...  0.49 us
  transfers between devices with their start and end apart: 10, of which 4 were waited for; matrix products, arithmetic and copies ran while one was open for 1% of the time, Pallas kernels for 21%

profile of v6, /device:TPU:0, one launch (start us, length us, event | category | flops | bytes accessed | tf_op | source)
XLA Modules:
  0.0 23.5 jit_solution(8632536288588884022)
XLA Ops:
  0.0 3.0 %collective-permute-start.1 = (bf16[128,512]{1,0:T(8,128)(2,1)}, bf16[128,512]{1,0:T(8,128)(2,1)S(1)}, u32[]{:S(2)}, u32[]{:S(2)}) collective-permute-start(bf16[128,512]{1,0:T(8,128)(2,1)} %tokens.1), channel_id=1, source_target_pairs={{0,2},{1,3},{2,0},{3,1},{4,6},{5,7},{6,4},{7,5},{8,10},{9,11},{10,... | collective-permute-start | bytes 393224 | tf_op jit(solution)/shard_map/ppermute | solution.py:376
  3.0 0.0 collective-permute-start
  3.0 2.1 %load.1 = (bf16[128,512]{1,0:T(8,128)(2,1)S(1)}, f32[1,2048]{1,0:T(1,128)S(1)}, bf16[2048,256]{1,0:T(8,128)(2,1)S(1)}, bf16[2048,512]{1,0:T(8,128)(2,1)S(1)}, s32[1,128]{1,0:T(1,128)S(1)}) custom-call(bf16[128,512]{1,0:T(8,128)(2,1)} %tokens.1, f32[1,2048]{1,0:T(1,128)} %bitcast.2, bf16[2048,256]{1,0:T(8,128)(2,1)} %key_weight.1, ...), custom_call_target="tpu_custom_call" | custom-call | tf_op jit(solution)/shard_map/load/pallas_call | solution.py:381
  5.1 0.0 copy-start
  5.1 0.0 copy-start.1
  5.1 1.6 %collective-permute-done.1.refs_2_.x2 = bf16[128,512]{1,0:T(8,128)(2,1)S(1)} collective-permute-done((bf16[128,512]{1,0:T(8,128)(2,1)}, bf16[128,512]{1,0:T(8,128)(2,1)S(1)}, u32[]{:S(2)}, u32[]{:S(2)}) %collective-permute-start.1) | collective-permute-done | bytes 131104 | tf_op jit(solution)/shard_map/ppermute | solution.py:376
  6.7 0.0 collective-permute-start.2
  6.7 0.3 %multiply_sine_fusion = (f32[128,64]{1,0:T(8,128)S(1)}, f32[128,64]{1,0:T(8,128)S(1)}) fusion(f32[64]{0:T(128)S(1)} %multiply_power_fusion, f32[128]{0:T(128)S(1)} %add_convert_fusion), kind=kLoop, calls=%fused_computation | loop fusion | flops 8192 | bytes 66304 | tf_op jit(solution)/shard_map/sin | solution.py:412
  7.0 0.0 collective-permute-done.refs_1_.x1
  7.0 0.1 squares.1
  7.1 0.9 %collective-permute-done.2.x3 = bf16[128,512]{1,0:T(8,128)(2,1)S(1)} collective-permute-done((bf16[128,512]{1,0:T(8,128)(2,1)S(1)}, bf16[128,512]{1,0:T(8,128)(2,1)S(1)}, u32[]{:S(2)}, u32[]{:S(2)}) %collective-permute-start.2) | collective-permute-done | bytes 131104 | tf_op jit(solution)/shard_map/ppermute | solution.py:376
  8.0 0.5 %keys_values.1 = (bf16[128,256]{1,0:T(8,128)(2,1)S(1)}, bf16[128,2048]{1,0:T(8,128)(2,1)S(1)}) custom-call(f32[128,128]{1,0:T(8,128)S(1)} %squares.1, bf16[128,512]{1,0:T(8,128)(2,1)S(1)} %get-tuple-element.23.refs_0_.x0, bf16[128,512]{1,0:T(8,128)(2,1)S(1)} %collective-permute-done.refs_1_.x1, bf16[128,512]{1,0:T(8,128)(2,1)S(1)} %collective-permute-done.1.refs_2_.x2, ...), custom_call_target="tpu_custom_call" | custom-call | tf_op jit(solution)/shard_map/keys_values/pallas_call | solution.py:423
  8.5 2.9 %collective-permute-start.4 = (bf16[128,256]{1,0:T(8,128)(2,1)S(1)}, bf16[128,256]{1,0:T(8,128)(2,1)S(1)}, u32[]{:S(2)}, u32[]{:S(2)}) collective-permute-start(bf16[128,256]{1,0:T(8,128)(2,1)S(1)} %get-tuple-element.29.own), channel_id=1, source_target_pairs={{0,16},{1,25},{2,18},{3,27},{4,20},{5,29},{6,22},{7,31},{8,24},{9,... | collective-permute-start | bytes 196616 | tf_op jit(solution)/shard_map/ppermute | solution.py:376
  11.4 1.5 %collective-permute-start.3 = (bf16[128,256]{1,0:T(8,128)(2,1)S(1)}, bf16[128,256]{1,0:T(8,128)(2,1)S(1)}, u32[]{:S(2)}, u32[]{:S(2)}) collective-permute-start(bf16[128,256]{1,0:T(8,128)(2,1)S(1)} %get-tuple-element.29.own), channel_id=1, source_target_pairs={{0,4},{1,9},{2,6},{3,11},{4,0},{5,13},{6,2},{7,15},{8,12},{9,1},{1... | collective-permute-start | bytes 196616 | tf_op jit(solution)/shard_map/ppermute | solution.py:376
  12.9 0.1 collective-permute-start.7
  13.0 2.1 %collective-permute-done.4.refs_4_ = bf16[128,256]{1,0:T(8,128)(2,1)S(1)} collective-permute-done((bf16[128,256]{1,0:T(8,128)(2,1)S(1)}, bf16[128,256]{1,0:T(8,128)(2,1)S(1)}, u32[]{:S(2)}, u32[]{:S(2)}) %collective-permute-start.4) | collective-permute-done | bytes 65568 | tf_op jit(solution)/shard_map/ppermute | solution.py:376
  15.1 0.0 collective-permute-start.6
  15.1 0.6 %collective-permute-done.3.refs_3_ = bf16[128,256]{1,0:T(8,128)(2,1)S(1)} collective-permute-done((bf16[128,256]{1,0:T(8,128)(2,1)S(1)}, bf16[128,256]{1,0:T(8,128)(2,1)S(1)}, u32[]{:S(2)}, u32[]{:S(2)}) %collective-permute-start.3) | collective-permute-done | bytes 65568 | tf_op jit(solution)/shard_map/ppermute | solution.py:376
  15.7 0.1 collective-permute-start.5
  15.8 3.6 %collective-permute-start.8 = (bf16[128,256]{1,0:T(8,128)(2,1)S(1)}, bf16[128,256]{1,0:T(8,128)(2,1)S(1)}, u32[]{:S(2)}, u32[]{:S(2)}) collective-permute-start(bf16[128,256]{1,0:T(8,128)(2,1)S(1)} %get-tuple-element.29.own), channel_id=1, source_target_pairs={{0,12},{1,13},{2,14},{3,15},{4,8},{5,9},{6,10},{7,11},{8,4},{9,5},... | collective-permute-start | bytes 196616 | tf_op jit(solution)/shard_map/ppermute | solution.py:376
  19.4 0.0 collective-permute-done.7.refs_5_
  19.5 0.0 collective-permute-start.9
  19.5 0.0 copy-done
  19.5 0.0 copy-done.1
  19.5 1.6 %queries.1 = (bf16[512,128]{1,0:T(8,128)(2,1)S(1)}, f32[128,1024]{1,0:T(8,128)S(1)}, f32[512,128]{1,0:T(8,128)S(1)}, f32[512,128]{1,0:T(8,128)S(1)}, f32[512,128]{1,0:T(8,128)S(1)}) custom-call(s32[8]{0:T(128)S(1)} %copy-done, s32[1,2]{1,0:T(1,128)S(1)} %copy-done.1, bf16[128,2048]{1,0:T(8,128)(2,1)S(1)} %get-tuple-element.26.normed, ...), custom_call_target="tpu_custom_call" | custom-call | tf_op jit(solution)/shard_map/queries/pallas_call | solution.py:477
  21.1 0.5 %shard_map.82 = (f32[512,128]{1,0:T(8,128)S(1)}, f32[512,128]{1,0:T(8,128)S(1)}, f32[512,128]{1,0:T(8,128)S(1)}) custom-call(bf16[512,128]{1,0:T(8,128)(2,1)S(1)} %get-tuple-element.30.q, f32[128,1024]{1,0:T(8,128)S(1)} %get-tuple-element.31.bias, f32[512,128]{1,0:T(8,128)S(1)} %get-tuple-element.32.refs_0_, f32[512,128]{1,0:T(8,128)S(1)} %get-tuple-element.33.refs_1_, ...), custom_call_target="tpu_custom_call" | custom-call | tf_op jit(solution)/shard_map/pallas_call | solution.py:505
  21.6 0.0 collective-permute-done.6.refs_4_
  21.7 0.0 collective-permute-done.5.refs_3_
  21.7 0.6 %shard_map.83 = (f32[512,128]{1,0:T(8,128)S(1)}, f32[512,128]{1,0:T(8,128)S(1)}, f32[512,128]{1,0:T(8,128)S(1)}) custom-call(bf16[512,128]{1,0:T(8,128)(2,1)S(1)} %get-tuple-element.30.q, f32[128,1024]{1,0:T(8,128)S(1)} %get-tuple-element.31.bias, f32[512,128]{1,0:T(8,128)S(1)} %get-tuple-element.35.refs_0_, f32[512,128]{1,0:T(8,128)S(1)} %get-tuple-element.36.refs_1_, ...), custom_call_target="tpu_custom_call" | custom-call | tf_op jit(solution)/shard_map/pallas_call | solution.py:505
  22.3 0.0 collective-permute-done.8.refs_3_
  22.3 0.0 collective-permute-done.9.refs_4_
  22.3 1.2 %last.1 = bf16[128,512]{1,0:T(8,128)(2,1)} custom-call(bf16[512,128]{1,0:T(8,128)(2,1)S(1)} %get-tuple-element.30.q, f32[128,1024]{1,0:T(8,128)S(1)} %get-tuple-element.31.bias, f32[512,128]{1,0:T(8,128)S(1)} %get-tuple-element.38.refs_0_, f32[512,128]{1,0:T(8,128)S(1)} %get-tuple-element.39.refs_1_, f32[512,128]{1,0:T(8,128)S(1)} %get-tuple-element.40.refs_2_, ...), custom_call_target="tpu_custom_call" | custom-call | tf_op jit(solution)/shard_map/last/pallas_call | solution.py:513
  (2 shorter events, 0.0 us)
Async XLA Ops:
  0.0 6.7 %collective-permute-start.1 = (bf16[128,512]{1,0:T(8,128)(2,1)}, bf16[128,512]{1,0:T(8,128)(2,1)S(1)}, u32[]{:S(2)}, u32[]{:S(2)}) collective-permute-start(bf16[128,512]{1,0:T(8,128)(2,1)} %tokens.1), channel_id=1, source_target_pairs={{0,2},{1,3},{2,0},{3,1},{4,6},{5,7},{6,4},{7,5},{8,10},{9,11},{10,... | collective-permute-start | bytes 393224 | tf_op jit(solution)/shard_map/ppermute | solution.py:376
  3.0 4.0 %collective-permute-start = (bf16[128,512]{1,0:T(8,128)(2,1)}, bf16[128,512]{1,0:T(8,128)(2,1)S(1)}, u32[]{:S(2)}, u32[]{:S(2)}) collective-permute-start(bf16[128,512]{1,0:T(8,128)(2,1)} %tokens.1), channel_id=1, source_target_pairs={{0,1},{1,0},{2,3},{3,2},{4,5},{5,4},{6,7},{7,6},{8,9},{9,8},{10,11... | collective-permute-start | bytes 393224 | tf_op jit(solution)/shard_map/ppermute | solution.py:376
  5.1 14.4 %copy-start = (s32[8]{0:T(128)S(1)}, s32[8]{0:T(128)}, u32[]{:S(2)}) copy-start(s32[8]{0:T(128)} %lengths.1) | copy-start | bytes 100
  5.1 14.4 %copy-start.1 = (s32[1,2]{1,0:T(1,128)S(1)}, s32[1,2]{1,0:T(1,128)}, u32[]{:S(2)}) copy-start(s32[1,2]{1,0:T(1,128)} %spans.1) | copy-start | bytes 28
  6.7 1.3 %collective-permute-start.2 = (bf16[128,512]{1,0:T(8,128)(2,1)S(1)}, bf16[128,512]{1,0:T(8,128)(2,1)S(1)}, u32[]{:S(2)}, u32[]{:S(2)}) collective-permute-start(bf16[128,512]{1,0:T(8,128)(2,1)S(1)} %collective-permute-done.1.refs_2_.x2), channel_id=1, source_target_pairs={{0,1},{1,0},{2,3},{3,2},{4,5},{5,4},{6,7},{7,6},{8,9},{9,8},{10,11... | collective-permute-start | bytes 393224 | tf_op jit(solution)/shard_map/ppermute | solution.py:376
  8.5 6.5 %collective-permute-start.4 = (bf16[128,256]{1,0:T(8,128)(2,1)S(1)}, bf16[128,256]{1,0:T(8,128)(2,1)S(1)}, u32[]{:S(2)}, u32[]{:S(2)}) collective-permute-start(bf16[128,256]{1,0:T(8,128)(2,1)S(1)} %get-tuple-element.29.own), channel_id=1, source_target_pairs={{0,16},{1,25},{2,18},{3,27},{4,20},{5,29},{6,22},{7,31},{8,24},{9,... | collective-permute-start | bytes 196616 | tf_op jit(solution)/shard_map/ppermute | solution.py:376
  11.4 4.3 %collective-permute-start.3 = (bf16[128,256]{1,0:T(8,128)(2,1)S(1)}, bf16[128,256]{1,0:T(8,128)(2,1)S(1)}, u32[]{:S(2)}, u32[]{:S(2)}) collective-permute-start(bf16[128,256]{1,0:T(8,128)(2,1)S(1)} %get-tuple-element.29.own), channel_id=1, source_target_pairs={{0,4},{1,9},{2,6},{3,11},{4,0},{5,13},{6,2},{7,15},{8,12},{9,1},{1... | collective-permute-start | bytes 196616 | tf_op jit(solution)/shard_map/ppermute | solution.py:376
  12.9 6.5 %collective-permute-start.7 = (bf16[128,256]{1,0:T(8,128)(2,1)S(1)}, bf16[128,256]{1,0:T(8,128)(2,1)S(1)}, u32[]{:S(2)}, u32[]{:S(2)}) collective-permute-start(bf16[128,256]{1,0:T(8,128)(2,1)S(1)} %get-tuple-element.29.own), channel_id=1, source_target_pairs={{0,20},{1,29},{2,22},{3,31},{4,16},{5,25},{6,18},{7,27},{8,28},{9,... | collective-permute-start | bytes 196616 | tf_op jit(solution)/shard_map/ppermute | solution.py:376
  15.1 6.6 %collective-permute-start.6 = (bf16[128,256]{1,0:T(8,128)(2,1)S(1)}, bf16[128,256]{1,0:T(8,128)(2,1)S(1)}, u32[]{:S(2)}, u32[]{:S(2)}) collective-permute-start(bf16[128,256]{1,0:T(8,128)(2,1)S(1)} %collective-permute-done.4.refs_4_), channel_id=1, source_target_pairs={{0,1},{1,0},{2,3},{3,2},{4,5},{5,4},{6,7},{7,6},{8,9},{9,8},{10,11... | collective-permute-start | bytes 196616 | tf_op jit(solution)/shard_map/ppermute | solution.py:376
  15.7 6.0 %collective-permute-start.5 = (bf16[128,256]{1,0:T(8,128)(2,1)S(1)}, bf16[128,256]{1,0:T(8,128)(2,1)S(1)}, u32[]{:S(2)}, u32[]{:S(2)}) collective-permute-start(bf16[128,256]{1,0:T(8,128)(2,1)S(1)} %collective-permute-done.3.refs_3_), channel_id=1, source_target_pairs={{0,1},{1,0},{2,3},{3,2},{4,5},{5,4},{6,7},{7,6},{8,9},{9,8},{10,11... | collective-permute-start | bytes 196616 | tf_op jit(solution)/shard_map/ppermute | solution.py:376
  15.8 6.5 %collective-permute-start.8 = (bf16[128,256]{1,0:T(8,128)(2,1)S(1)}, bf16[128,256]{1,0:T(8,128)(2,1)S(1)}, u32[]{:S(2)}, u32[]{:S(2)}) collective-permute-start(bf16[128,256]{1,0:T(8,128)(2,1)S(1)} %get-tuple-element.29.own), channel_id=1, source_target_pairs={{0,12},{1,13},{2,14},{3,15},{4,8},{5,9},{6,10},{7,11},{8,4},{9,5},... | collective-permute-start | bytes 196616 | tf_op jit(solution)/shard_map/ppermute | solution.py:376
  19.5 2.8 %collective-permute-start.9 = (bf16[128,256]{1,0:T(8,128)(2,1)S(1)}, bf16[128,256]{1,0:T(8,128)(2,1)S(1)}, u32[]{:S(2)}, u32[]{:S(2)}) collective-permute-start(bf16[128,256]{1,0:T(8,128)(2,1)S(1)} %collective-permute-done.7.refs_5_), channel_id=1, source_target_pairs={{0,1},{1,0},{2,3},{3,2},{4,5},{5,4},{6,7},{7,6},{8,9},{9,8},{10,11... | collective-permute-start | bytes 196616 | tf_op jit(solution)/shard_map/ppermute | solution.py:376
